TPU v7x, 256 devices: a whole 4x4x8 slice. The times are simulated.
256 devices in a mesh: strip: 8 (over y, core), cell: 32 (over x, z).
Axes of the slice: x: 4, y: 4, z: 8, core: 2. Of those that a mesh axis runs over, the one named last changes fastest.
Arguments:
- features: bfloat16 [65536, 256], P(('strip', 'cell')), may hold values from -6 to 6
- pair_atom: int32 [1048576], P(('strip', 'cell')), may hold values from 0 to 255
- partner_row: int32 [1048576], P(('strip', 'cell')), may hold values from 0 to 1535, as said below
- transpose_slot: int32 [1048576], P(('strip', 'cell')), may hold values from 0 to 6143, as said below
- distance: float32 [1048576], P(('strip', 'cell')), may hold values from 1 to 8
- send_rows: int32 [8192, 48], P(('strip', 'cell')), may hold values from 0 to 767, as said below
- w_left: bfloat16 [256, 256], replicated, may hold values from -0.375 to 0.375
- w_right: bfloat16 [256, 256], replicated, may hold values from -0.375 to 0.375
- w_radial_in: bfloat16 [128, 256], replicated, may hold values from -4 to 4
- w_radial_out: bfloat16 [256, 256], replicated, may hold values from -0.375 to 0.375
- w_mix: bfloat16 [256, 256], replicated, may hold values from -0.375 to 0.375
- w_out: bfloat16 [256, 169], replicated, may hold values from -0.375 to 0.375
Outputs:
- own_blocks: bfloat16 [169, 1048576], P(None, ('strip', 'cell'))
- partner_blocks: bfloat16 [169, 1572864], P(None, ('strip', 'cell'))
Inputs may be any that keep to these rules, and one draw needn't show every extreme that they name: `transpose_slot`: within one device the values are distinct; at most 64 of them share t // 64, and on every device one such group holds exactly 64. For pair slot p with transpose_slot t: partner_row // 48 equals (t // 64) % 32, and partner_row % 3 equals t // 2048. `send_rows`: entry k lies in [(k % 3) * 256, (k % 3 + 1) * 256); part k % 3 names the device of strip s - 1, s, s + 1 (cyclic) with the same cell index.
All inputs are finite; a program needn't handle non-finite values.
Results may differ from a plain program's by a relative error of at most 0.0084.
Values may be sent and summed in bfloat16 or wider, within the bound.
A program may use at most 64 MiB of HBM per device.

v0:
```python
import jax
import jax.numpy as jnp
import numpy as np
from jax import lax
from jax.sharding import PartitionSpec as P

cutoff = 8.0


def padded(cells, sides, width):
    for axis, dim in sides:
        count = lax.axis_size(axis)
        head = lax.slice_in_dim(cells, 0, width, axis=dim)
        tail = lax.slice_in_dim(cells, cells.shape[dim] - width, cells.shape[dim], axis=dim)
        cells = jnp.concatenate(
            [
                lax.ppermute(tail, axis, [(i, (i + 1) % count) for i in range(count)]),
                cells,
                lax.ppermute(head, axis, [((i + 1) % count, i) for i in range(count)]),
            ],
            axis=dim,
        )
    return cells


def passed_along(x, axis, by):
    peers = lax.axis_size(axis)
    return lax.ppermute(x, axis, [(i, (i + by) % peers) for i in range(peers)])


def radial_basis(distance, count):
    centers = jnp.arange(count, dtype=jnp.float32) * (cutoff / (count - 1))
    spacing = 2.0 * cutoff / count
    scaled = (distance[:, None] - centers[None, :]) / spacing
    envelope = 0.5 * (jnp.cos(jnp.pi * distance / cutoff) + 1.0)
    return (jnp.exp(-scaled * scaled) * envelope[:, None]).astype(jnp.bfloat16)


def select_rows(index, table):
    picker = (index[:, None] == jnp.arange(table.shape[0], dtype=jnp.int32)[None, :]).astype(
        jnp.bfloat16
    )
    return jnp.dot(picker, table, preferred_element_type=jnp.float32).astype(jnp.bfloat16)


def body(
    features,
    pair_atom,
    partner_row,
    transpose_slot,
    distance,
    send_rows,
    w_left,
    w_right,
    w_radial_in,
    w_radial_out,
    w_mix,
    w_out,
):
    atom_count = features.shape[0]
    width = features.shape[1]
    cells = lax.axis_size("cell")
    extended = padded(features[None], (("strip", 0),), 1)
    nearby = extended.reshape(3 * atom_count, width)
    every, lists = (
        lax.all_gather(nearby[None], "cell", axis=0, tiled=True),
        lax.all_gather(send_rows[None], "cell", axis=0, tiled=True),
    )
    myself = lax.axis_index("cell")
    mine = lax.dynamic_index_in_dim(lists, myself, 1, keepdims=False)
    fetched = every[jnp.arange(cells, dtype=jnp.int32)[:, None], mine]
    fetched = fetched.reshape(-1, width)
    left = jnp.dot(features, w_left, preferred_element_type=jnp.float32).astype(jnp.bfloat16)
    right = jnp.dot(fetched, w_right, preferred_element_type=jnp.float32).astype(jnp.bfloat16)
    left_rows = select_rows(pair_atom, left)
    right_rows = select_rows(partner_row, right)
    basis = radial_basis(distance, w_radial_in.shape[0])
    radial = jax.nn.silu(jnp.dot(basis, w_radial_in, preferred_element_type=jnp.float32)).astype(
        jnp.bfloat16
    )
    gate = jnp.dot(radial, w_radial_out, preferred_element_type=jnp.float32)
    edge = (left_rows.astype(jnp.float32) * right_rows.astype(jnp.float32) * gate).astype(
        jnp.bfloat16
    )
    mixed = jax.nn.silu(jnp.dot(edge, w_mix, preferred_element_type=jnp.float32)).astype(
        jnp.bfloat16
    )
    own_blocks = lax.dot_general(
        w_out, mixed, (((0,), (1,)), ((), ())), preferred_element_type=jnp.float32
    ).astype(jnp.bfloat16)
    entries = w_out.shape[1]
    orbitals = int(np.sqrt(entries) + 0.5)
    order = np.arange(entries).reshape(orbitals, orbitals).T.reshape(-1)
    w_flipped = w_out[:, order]
    slot_total = 3 * cells * (pair_atom.shape[0] // (2 * cells))
    placed = jnp.zeros((slot_total, width), jnp.bfloat16).at[transpose_slot].set(mixed)
    outbox = lax.dot_general(
        w_flipped, placed, (((0,), (1,)), ((), ())), preferred_element_type=jnp.float32
    ).astype(jnp.bfloat16)
    outbox = outbox.reshape(entries, 3, slot_total // 3)
    arrived = lax.all_to_all(outbox, "cell", split_axis=2, concat_axis=2, tiled=True)
    pieces = [None, arrived[:, 1], None]
    for which, offset in ((0, -1), (2, 1)):
        pieces[which] = passed_along(arrived[:, which], "strip", offset)
    gathered = jnp.stack(pieces, 1)
    partner_blocks = gathered.reshape(entries, slot_total)
    return (own_blocks, partner_blocks)


def solution(mesh):
    in_specs = (
        P(("strip", "cell"), None),
        P(("strip", "cell")),
        P(("strip", "cell")),
        P(("strip", "cell")),
        P(("strip", "cell")),
        P(("strip", "cell"), None),
        P(),
        P(),
        P(),
        P(),
        P(),
        P(),
    )
    out_specs = (P(None, ("strip", "cell")), P(None, ("strip", "cell")))
    return jax.shard_map(body, mesh=mesh, in_specs=in_specs, out_specs=out_specs, check_vma=False)
```

profile of v0, /device:TPU:1, one launch (start us, length us, event | category | flops | bytes accessed | tf_op | source)
XLA Modules:
  0.0 328.8 jit_solution(13656995187292793223)
XLA Ops:
  7.3 2.7 collective-permute-start
  12.2 2.6 collective-permute-done.1
  16.6 43.2 %all-gather = s32[1024,48]{1,0:T(8,128)S(1)} all-gather(s32[32,48]{1,0:T(8,128)} %param.19), channel_id=2, replica_groups=mesh['strip'=8,'cell'=32] {'cell'}, dimensions={0}, use_global_device_ids=true | all-gather | bytes 202752 | tf_op jit(solution)/shard_map/all_gather | solution.py:67
  62.5 2.9 fusion.5
  65.4 4.4 %multiply_convert_fusion.1 = bf16[4096,256]{1,0:T(8,128)(2,1)} fusion(bf16[128,256]{1,0:T(8,128)(2,1)S(1)} %copy-done.10, f32[4096]{0:T(1024)S(1)} %add_multiply_fusion, f32[128]{0:T(128)S(1)} %iota_multiply_fusion, f32[4096]{0:T(1024)S(1)} %copy-done.6), kind=kOutput, calls=%fused_computation.17 | convolution fusion | flops 276824064 | bytes 2195968 | tf_op jit(solution)/shard_map/dot_general | solution.py:78
  69.8 67.2 %all-gather.3.cloned.1.call-done = bf16[32,768,256]{2,1,0:T(8,128)(2,1)} async-done(((bf16[1,768,256]{2,1,0:T(8,128)(2,1)}), bf16[32,768,256]{2,1,0:T(8,128)(2,1)}) %all-gather.3.cloned.1.call-update) | async-done | bytes 12582928 | tf_op jit(solution)/shard_map/all_gather | solution.py:66
  137.0 18.8 %gather_fusion = bf16[1536,256]{1,0:T(8,128)(2,1)S(1)} fusion(bf16[32,768,256]{2,1,0:T(8,128)(2,1)} %all-gather.3.cloned.1.call-done, s32[1536]{0:T(1024)S(1)} %reshape.54), kind=kCustom, calls=%fused_computation | custom fusion | bytes 1585152 | tf_op jit(solution)/shard_map/gather | solution.py:71
  155.9 9.3 %fusion.4 = f32[4096,256]{1,0:T(8,128)} fusion(f32[4096,256]{1,0:T(8,128)} %fusion.5, s32[4096]{0:T(1024)S(1)} %copy-done.11, bf16[1536,256]{1,0:T(8,128)(2,1)S(1)} %gather_fusion, bf16[256,256]{1,0:T(8,128)(2,1)S(1)} %copy-done.7), kind=kOutput, calls=%fused_computation.10 | convolution fusion | flops 3432382464 | bytes 9322496 | tf_op jit(solution)/shard_map/dot_general | solution.py:43
  165.2 5.6 %multiply_convert_fusion = bf16[4096,256]{1,0:T(8,128)(2,1)} fusion(bf16[256,256]{1,0:T(8,128)(2,1)S(1)} %copy-done.8, f32[4096,256]{1,0:T(8,128)} %fusion.4, bf16[4096,256]{1,0:T(8,128)(2,1)} %multiply_convert_fusion.1, bf16[256,256]{1,0:T(8,128)(2,1)S(1)} %copy-done.9), kind=kOutput, calls=%fused_computation.16 | convolution fusion | flops 1081081856 | bytes 8650752 | tf_op jit(solution)/shard_map/dot_general | solution.py:85
  170.8 19.5 %scatter_custom_fusion = bf16[6144,256]{1,0:T(8,128)(2,1)S(1)} fusion(s32[4096]{0:T(1024)S(1)} %compare_select_fusion, bf16[4096,256]{1,0:T(8,128)(2,1)} %multiply_convert_fusion, bf16[]{:T(256)} %constant.42.clone.1), kind=kCustom, calls=%fused_computation.27 | custom fusion | bytes 3146240 | tf_op jit(solution)/shard_map/scatter | solution.py:96
  190.3 2.5 convolution_convert_fusion
  192.9 5.9 %reshape.52 = bf16[169,3,2048]{2,1,0:T(4,128)(2,1)S(1)} reshape(bf16[169,6144]{1,0:T(8,128)(2,1)} %convolution_convert_fusion) | data formatting | bytes 4153344 | tf_op jit(solution)/shard_map/reshape | solution.py:100
  198.8 7.6 %copy.29 = bf16[169,3,2048]{0,1,2:T(4,128)(2,1)} copy(bf16[169,3,2048]{2,1,0:T(4,128)(2,1)S(1)} %reshape.52) | data formatting | bytes 4153344 | tf_op jit(solution)/shard_map/reshape | solution.py:100
  206.4 7.9 %reshape.81 = bf16[32,2,16224]{2,1,0:T(2,128)(2,1)S(1)} reshape(bf16[2048,3,169]{2,1,0:T(4,128)(2,1)} %bitcast.30) | data formatting | bytes 4153344
  214.2 52.4 %all_to_all.5 = bf16[32,2,16224]{2,1,0:T(2,128)(2,1)} all-to-all(bf16[32,2,16224]{2,1,0:T(2,128)(2,1)S(1)} %reshape.81), channel_id=1, replica_groups=mesh['strip'=8,'cell'=32] {'cell'}, dimensions={0} | all-to-all | bytes 4153344 | tf_op jit(solution)/shard_map/all_to_all | solution.py:101
  266.7 10.4 %reshape.82 = bf16[2048,3,169]{2,1,0:T(4,128)(2,1)} reshape(bf16[32,2,16224]{2,1,0:T(2,128)(2,1)} %all_to_all.5) | data formatting | bytes 4153344
  277.0 11.1 %fusion.24 = (bf16[169,1,2048]{0,1,2:T(2,128)(2,1)}, bf16[169,1,2048]{0,1,2:T(2,128)(2,1)S(1)}, bf16[169,1,2048]{0,1,2:T(2,128)(2,1)}) fusion(bf16[169,3,2048]{0,1,2:T(4,128)(2,1)} %bitcast.29), kind=kLoop, calls=%fused_computation.45 | loop fusion | bytes 4153344 | tf_op jit(solution)/shard_map/slice | solution.py:104
  288.1 5.8 %copy.34 = bf16[169,1,2048]{2,0,1:T(8,128)(2,1)} copy(bf16[169,1,2048]{0,1,2:T(2,128)(2,1)} %get-tuple-element.2) | data formatting | bytes 1384448
  293.8 4.7 %collective-permute-start.2 = (bf16[169,2048]{1,0:T(8,128)(2,1)}, bf16[169,2048]{1,0:T(8,128)(2,1)}, u32[]{:S(2)}, u32[]{:S(2)}) collective-permute-start(bf16[169,2048]{1,0:T(8,128)(2,1)} %bitcast.5), channel_id=1, source_target_pairs={{0,224},{32,0},{64,32},{96,64},{128,96},{160,128},{192,160},{224,1... | collective-permute-start | bytes 2076680 | tf_op jit(solution)/shard_map/ppermute | solution.py:28
  298.5 5.7 %copy.36 = bf16[169,1,2048]{2,0,1:T(8,128)(2,1)} copy(bf16[169,1,2048]{0,1,2:T(2,128)(2,1)} %get-tuple-element.4) | data formatting | bytes 1384448
  305.4 3.5 %fusion.7 = bf16[169,4096]{1,0:T(8,128)(2,1)} fusion(bf16[4096,256]{1,0:T(8,128)(2,1)} %multiply_convert_fusion, bf16[256,169]{0,1:T(8,128)(2,1)S(1)} %copy-done.2), kind=kOutput, calls=%fused_computation.15 | convolution fusion | flops 355110912 | bytes 3568128 | tf_op jit(solution)/shard_map/dot_general | solution.py:88
  310.2 3.8 %collective-permute-done.3 = bf16[169,2048]{1,0:T(8,128)(2,1)} collective-permute-done((bf16[169,2048]{1,0:T(8,128)(2,1)}, bf16[169,2048]{1,0:T(8,128)(2,1)}, u32[]{:S(2)}, u32[]{:S(2)}) %collective-permute-start.3) | collective-permute-done | bytes 692256 | tf_op jit(solution)/shard_map/ppermute | solution.py:28
  315.5 1.8 copy.33
  318.8 3.2 copy.37
  (42 shorter events, 12.1 us)
Async XLA Ops:
  7.2 55.3 %copy-start = (bf16[256,256]{1,0:T(8,128)(2,1)S(1)}, bf16[256,256]{1,0:T(8,128)(2,1)}, u32[]{:S(2)}) copy-start(bf16[256,256]{1,0:T(8,128)(2,1)} %param.20) | copy-start | bytes 393220
  7.2 55.3 %copy-start.3 = (bf16[256,256]{1,0:T(8,128)(2,1)S(1)}, bf16[256,256]{1,0:T(8,128)(2,1)}, u32[]{:S(2)}) copy-start(bf16[256,256]{1,0:T(8,128)(2,1)} %param.14) | copy-start | bytes 393220
  7.2 55.2 %copy-start.6 = (f32[4096]{0:T(1024)S(1)}, f32[4096]{0:T(1024)}, u32[]{:S(2)}) copy-start(f32[4096]{0:T(1024)} %param.18) | copy-start | bytes 49156
  7.2 55.2 %copy-start.5 = (s32[4096]{0:T(1024)S(1)}, s32[4096]{0:T(1024)}, u32[]{:S(2)}) copy-start(s32[4096]{0:T(1024)} %param.17) | copy-start | bytes 49156
  7.2 55.3 %copy-start.4 = (s32[4096]{0:T(1024)S(1)}, s32[4096]{0:T(1024)}, u32[]{:S(2)}) copy-start(s32[4096]{0:T(1024)} %param.15) | copy-start | bytes 49156
  7.2 129.8 %all-gather.3.cloned.1.call-start = ((), (), s32[]{:S(2)}) async-start(), calls=%async_computation.1 | async-start | bytes 12976128 | tf_op jit(solution)/shard_map/all_gather | solution.py:66
  7.3 5.0 %collective-permute-start = (bf16[1,256,256]{2,1,0:T(8,128)(2,1)}, bf16[1,256,256]{2,1,0:T(8,128)(2,1)S(1)}, u32[]{:S(2)}, u32[]{:S(2)}) collective-permute-start(bf16[1,256,256]{2,1,0:T(8,128)(2,1)} %bitcast.35), channel_id=1, source_target_pairs={{0,32},{32,64},{64,96},{96,128},{128,160},{160,192},{192,224},{224... | collective-permute-start | bytes 393224 | tf_op jit(solution)/shard_map/ppermute | solution.py:17
  10.0 4.9 %collective-permute-start.1 = (bf16[1,256,256]{2,1,0:T(8,128)(2,1)}, bf16[1,256,256]{2,1,0:T(8,128)(2,1)S(1)}, u32[]{:S(2)}, u32[]{:S(2)}) collective-permute-start(bf16[1,256,256]{2,1,0:T(8,128)(2,1)} %bitcast.36), channel_id=1, source_target_pairs={{32,0},{64,32},{96,64},{128,96},{160,128},{192,160},{224,192},{0,2... | collective-permute-start | bytes 393224 | tf_op jit(solution)/shard_map/ppermute | solution.py:19
  60.6 4.8 %copy-start.10 = (bf16[128,256]{1,0:T(8,128)(2,1)S(1)}, bf16[128,256]{1,0:T(8,128)(2,1)}, u32[]{:S(2)}) copy-start(bf16[128,256]{1,0:T(8,128)(2,1)} %param.22) | copy-start | bytes 196612
  69.8 86.1 %copy-start.7 = (bf16[256,256]{1,0:T(8,128)(2,1)S(1)}, bf16[256,256]{1,0:T(8,128)(2,1)}, u32[]{:S(2)}) copy-start(bf16[256,256]{1,0:T(8,128)(2,1)} %param.21) | copy-start | bytes 393220
  69.8 86.1 %copy-start.11 = (s32[4096]{0:T(1024)S(1)}, s32[4096]{0:T(1024)}, u32[]{:S(2)}) copy-start(s32[4096]{0:T(1024)} %param.16) | copy-start | bytes 49156
  155.9 9.4 %copy-start.8 = (bf16[256,256]{1,0:T(8,128)(2,1)S(1)}, bf16[256,256]{1,0:T(8,128)(2,1)}, u32[]{:S(2)}) copy-start(bf16[256,256]{1,0:T(8,128)(2,1)} %param.24) | copy-start | bytes 393220
  155.9 9.4 %copy-start.9 = (bf16[256,256]{1,0:T(8,128)(2,1)S(1)}, bf16[256,256]{1,0:T(8,128)(2,1)}, u32[]{:S(2)}) copy-start(bf16[256,256]{1,0:T(8,128)(2,1)} %param.23) | copy-start | bytes 393220
  288.1 17.3 %copy-start.2 = (bf16[256,169]{0,1:T(8,128)(2,1)S(1)}, bf16[256,169]{0,1:T(8,128)(2,1)}, u32[]{:S(2)}) copy-start(bf16[256,169]{0,1:T(8,128)(2,1)} %param.25) | copy-start | bytes 259588
  293.8 16.3 %collective-permute-start.2 = (bf16[169,2048]{1,0:T(8,128)(2,1)}, bf16[169,2048]{1,0:T(8,128)(2,1)}, u32[]{:S(2)}, u32[]{:S(2)}) collective-permute-start(bf16[169,2048]{1,0:T(8,128)(2,1)} %bitcast.5), channel_id=1, source_target_pairs={{0,224},{32,0},{64,32},{96,64},{128,96},{160,128},{192,160},{224,1... | collective-permute-start | bytes 2076680 | tf_op jit(solution)/shard_map/ppermute | solution.py:28
  304.3 9.7 %collective-permute-start.3 = (bf16[169,2048]{1,0:T(8,128)(2,1)}, bf16[169,2048]{1,0:T(8,128)(2,1)}, u32[]{:S(2)}, u32[]{:S(2)}) collective-permute-start(bf16[169,2048]{1,0:T(8,128)(2,1)} %bitcast.7), channel_id=1, source_target_pairs={{0,32},{32,64},{64,96},{96,128},{128,160},{160,192},{192,224},{224... | collective-permute-start | bytes 2076680 | tf_op jit(solution)/shard_map/ppermute | solution.py:28
  317.3 4.7 %copy-start.1 = (bf16[256,256]{1,0:T(8,128)(2,1)S(1)}, bf16[256,256]{1,0:T(8,128)(2,1)}, u32[]{:S(2)}) copy-start(bf16[256,256]{1,0:T(8,128)(2,1)} %param.20) | copy-start | bytes 393220
Sparse Core Ops, SparseCore 0:
  16.7 120.2 all-gather.2
where the time goes:
time: 331 us; the launch traced here: 329 us
  local copies, waits for them, and re-layouts  102 us (31%)
  blocking collectives  95.6 us (29%)
  waiting for transfers between devices  75.4 us (23%)
  matrix products  28.3 us (9%)
  between operations  14.3 us (4%)
  starting transfers between devices  9.11 us (3%)
  other arithmetic  4.04 us (1%)
    all_gather x1, waiting for transfers between devices, body(): lax.all_gather(nearby[None], 'cell', axis=0, tiled=True)  67.2 us
    all_to_all x1, blocking collectives, body(): lax.all_to_all(outbox, 'cell', split_axis=2, concat_axis=2, tiled=True)  52.4 us
    all_gather x1, blocking collectives, body(): lax.all_gather(send_rows[None], 'cell', axis=0, tiled=True)  43.2 us
    unnamed x31, local copies, waits for them, and re-layouts  35.6 us
    scatter x1, local copies, waits for them, and re-layouts, body(): jnp.zeros((slot_total, width), jnp.bfloat16).at[transpose_slot].set(mixed)  19.5 us
    gather x1, local copies, waits for them, and re-layouts, body(): fetched = every[jnp.arange(cells, dtype=jnp.int32)[:, None], mine]  18.8 us
    reshape x2, local copies, waits for them, and re-layouts, body(): outbox = outbox.reshape(entries, 3, slot_total // 3)  13.5 us
    dot_general x2, matrix products, select_rows(): jnp.dot(picker, table, preferred_element_type=jnp.float32)  12.2 us
  transfers between devices with their start and end apart: 5, of which 4 were waited for; matrix products, arithmetic and copies ran while one was open for 6% of the time, Pallas kernels for 0%

commit v1 on v0

--- a/solution.py
+++ b/solution.py
@@ -5,22 +5,6 @@
 from jax.sharding import PartitionSpec as P
 
 cutoff = 8.0
-
-
-def padded(cells, sides, width):
-    for axis, dim in sides:
-        count = lax.axis_size(axis)
-        head = lax.slice_in_dim(cells, 0, width, axis=dim)
-        tail = lax.slice_in_dim(cells, cells.shape[dim] - width, cells.shape[dim], axis=dim)
-        cells = jnp.concatenate(
-            [
-                lax.ppermute(tail, axis, [(i, (i + 1) % count) for i in range(count)]),
-                cells,
-                lax.ppermute(head, axis, [((i + 1) % count, i) for i in range(count)]),
-            ],
-            axis=dim,
-        )
-    return cells
 
 
 def passed_along(x, axis, by):
@@ -57,21 +41,17 @@
     w_mix,
     w_out,
 ):
-    atom_count = features.shape[0]
     width = features.shape[1]
     cells = lax.axis_size("cell")
-    extended = padded(features[None], (("strip", 0),), 1)
-    nearby = extended.reshape(3 * atom_count, width)
-    every, lists = (
-        lax.all_gather(nearby[None], "cell", axis=0, tiled=True),
-        lax.all_gather(send_rows[None], "cell", axis=0, tiled=True),
+    left = jnp.dot(features, w_left, preferred_element_type=jnp.float32).astype(jnp.bfloat16)
+    right_own = jnp.dot(features, w_right, preferred_element_type=jnp.float32).astype(jnp.bfloat16)
+    tables = jnp.concatenate(
+        [passed_along(right_own, "strip", 1), right_own, passed_along(right_own, "strip", -1)], axis=0
     )
-    myself = lax.axis_index("cell")
-    mine = lax.dynamic_index_in_dim(lists, myself, 1, keepdims=False)
-    fetched = every[jnp.arange(cells, dtype=jnp.int32)[:, None], mine]
-    fetched = fetched.reshape(-1, width)
-    left = jnp.dot(features, w_left, preferred_element_type=jnp.float32).astype(jnp.bfloat16)
-    right = jnp.dot(fetched, w_right, preferred_element_type=jnp.float32).astype(jnp.bfloat16)
+    chosen = select_rows(send_rows.reshape(-1), tables)
+    right = lax.all_to_all(
+        chosen.reshape(cells, -1, width), "cell", split_axis=0, concat_axis=0, tiled=True
+    ).reshape(-1, width)
     left_rows = select_rows(pair_atom, left)
     right_rows = select_rows(partner_row, right)
     basis = radial_basis(distance, w_radial_in.shape[0])

time: 331 us -> 212 us (0.64)
  waiting for transfers between devices: 75.4 us -> 14.8 us
  blocking collectives: 95.6 us -> 50.9 us
  starting transfers between devices: 9.11 us -> 27.7 us
  local copies, waits for them, and re-layouts: 102 us -> 84.7 us
  between operations: 14.3 us -> 0.82 us
    all_gather x1 -> x0, waiting for transfers between devices: 67.2 us -> none  [body(): lax.all_gather(nearby[None], 'cell', axis=0, tiled=True)]
    all_gather x1 -> x0, blocking collectives: 43.2 us -> none  [body(): lax.all_gather(send_rows[None], 'cell', axis=0, tiled=True)]
    gather x1 -> x0, local copies, waits for them, and re-layouts: 18.8 us -> none  [body(): fetched = every[jnp.arange(cells, dtype=jnp.int32)[:, None], mine]]
    ppermute x2 -> x4, starting transfers between devices: 5.83 us -> 17 us  [passed_along(): return lax.ppermute(x, axis, [(i, (i + by) % peers) for i in range(peers)])]
    all_to_all x0 -> x1, starting transfers between devices: none -> 10.7 us  [body(): lax.all_to_all(chosen.reshape(cells, -1, width), 'cell', split_axis=0, co...]
    all_to_all x0 -> x1, waiting for transfers between devices: none -> 8.5 us  [body(): lax.all_to_all(chosen.reshape(cells, -1, width), 'cell', split_axis=0, co...]
    ppermute x2 -> x0, waiting for transfers between devices: 4.35 us -> none  [the longest x1 2.63 us: padded(): lax.ppermute(head, axis, [((i + 1) % count, i) for i in range(count)])]
    unnamed x31 -> x27, local copies, waits for them, and re-layouts: 35.6 us -> 36.5 us
  transfers between devices with their start and end apart: 5 -> 5, of which waited for: 4 -> 3; matrix products, arithmetic and copies ran while one was open for 6% -> 7% of each run, Pallas kernels for 0% -> 0%
where the time goes in v1:
time: 212 us; the launch traced here: 211 us
  local copies, waits for them, and re-layouts  84.7 us (40%)
  blocking collectives  50.9 us (24%)
  matrix products  29.7 us (14%)
  starting transfers between devices  27.7 us (13%)
  waiting for transfers between devices  14.8 us (7%)
  other arithmetic  2.34 us (1%)
    all_to_all x1, blocking collectives, body(): lax.all_to_all(outbox, 'cell', split_axis=2, concat_axis=2, tiled=True)  50.9 us
    unnamed x27, local copies, waits for them, and re-layouts  36.5 us
    scatter x1, local copies, waits for them, and re-layouts, body(): jnp.zeros((slot_total, width), jnp.bfloat16).at[transpose_slot].set(mixed)  19.5 us
    ppermute x4, starting transfers between devices, passed_along(): return lax.ppermute(x, axis, [(i, (i + by) % peers) for i in range(peers)])  17 us
    reshape x2, local copies, waits for them, and re-layouts, body(): outbox = outbox.reshape(entries, 3, slot_total // 3)  13.5 us
    dot_general x3, matrix products, select_rows(): jnp.dot(picker, table, preferred_element_type=jnp.float32)  12.6 us
    slice x1, local copies, waits for them, and re-layouts, body(): pieces[which] = passed_along(arrived[:, which], 'strip', offset)  11 us
    all_to_all x1, starting transfers between devices, body(): lax.all_to_all(chosen.reshape(cells, -1, width), 'cell', split_axis=0, co...  10.7 us
  transfers between devices with their start and end apart: 5, of which 3 were waited for; matrix products, arithmetic and copies ran while one was open for 7% of the time, Pallas kernels for 0%

profile of v1, /device:TPU:1, one launch (start us, length us, event | category | flops | bytes accessed | tf_op | source)
XLA Modules:
  0.0 210.9 jit_solution(13775485923931553958)
XLA Ops:
  2.6 3.2 %collective-permute-start.1 = (bf16[256,256]{1,0:T(8,128)(2,1)S(1)}, bf16[256,256]{1,0:T(8,128)(2,1)S(1)}, u32[]{:S(2)}, u32[]{:S(2)}) collective-permute-start(bf16[256,256]{1,0:T(8,128)(2,1)S(1)} %convolution_convert_fusion.3), channel_id=1, source_target_pairs={{0,224},{32,0},{64,32},{96,64},{128,96},{160,128},{192,160},{224,1... | collective-permute-start | bytes 393224 | tf_op jit(solution)/shard_map/ppermute | solution.py:12
  9.1 1.9 fusion.9
  11.0 10.7 %all-to-all-start = ((bf16[32,48,256]{2,1,0:T(8,128)(2,1)}), bf16[32,48,256]{2,1,0:T(8,128)(2,1)S(1)}, u32[]{:S(2)}, u32[]{:S(2)}) async-start(bf16[32,48,256]{2,1,0:T(8,128)(2,1)} %bitcast), calls=%async_computation | async-start | bytes 1572864 | tf_op jit(solution)/shard_map/all_to_all | solution.py:52
  21.8 2.9 %fusion.5 = f32[4096,256]{1,0:T(8,128)} fusion(s32[4096]{0:T(1024)S(1)} %copy-done.3, bf16[256,256]{1,0:T(8,128)(2,1)S(1)} %copy-done, bf16[256,256]{1,0:T(8,128)(2,1)S(1)} %copy-done.2), kind=kOutput, calls=%fused_computation.11 | convolution fusion | flops 573636608 | bytes 4472832 | tf_op jit(solution)/shard_map/dot_general | solution.py:27
  24.7 4.4 %multiply_convert_fusion.1 = bf16[4096,256]{1,0:T(8,128)(2,1)} fusion(bf16[128,256]{1,0:T(8,128)(2,1)S(1)} %copy-done.8, f32[4096]{0:T(1024)S(1)} %add_multiply_fusion, f32[128]{0:T(128)S(1)} %iota_multiply_fusion, f32[4096]{0:T(1024)S(1)} %copy-done.5), kind=kOutput, calls=%fused_computation.18 | convolution fusion | flops 276824064 | bytes 2195968 | tf_op jit(solution)/shard_map/dot_general | solution.py:58
  29.2 8.5 %all-to-all-done = bf16[32,48,256]{2,1,0:T(8,128)(2,1)S(1)} async-done(((bf16[32,48,256]{2,1,0:T(8,128)(2,1)}), bf16[32,48,256]{2,1,0:T(8,128)(2,1)S(1)}, u32[]{:S(2)}, u32[]{:S(2)}) %all-to-all-start) | async-done | bytes 786464 | tf_op jit(solution)/shard_map/all_to_all | solution.py:52
  37.7 7.8 %fusion.4 = f32[4096,256]{1,0:T(8,128)} fusion(f32[4096,256]{1,0:T(8,128)} %fusion.5, bf16[1536,256]{1,0:T(8,128)(2,1)S(1)} %bitcast.31, s32[4096]{0:T(1024)S(1)} %copy-done.9), kind=kOutput, calls=%fused_computation.9 | convolution fusion | flops 3230662656 | bytes 9191424 | tf_op jit(solution)/shard_map/dot_general | solution.py:27
  45.5 5.5 %multiply_convert_fusion = bf16[4096,256]{1,0:T(8,128)(2,1)} fusion(bf16[256,256]{1,0:T(8,128)(2,1)S(1)} %copy-done.6, f32[4096,256]{1,0:T(8,128)} %fusion.4, bf16[4096,256]{1,0:T(8,128)(2,1)} %multiply_convert_fusion.1, bf16[256,256]{1,0:T(8,128)(2,1)S(1)} %copy-done.7), kind=kOutput, calls=%fused_computation.17 | convolution fusion | flops 1081081856 | bytes 8650752 | tf_op jit(solution)/shard_map/dot_general | solution.py:65
  51.1 19.5 %scatter_custom_fusion = bf16[6144,256]{1,0:T(8,128)(2,1)S(1)} fusion(s32[4096]{0:T(1024)S(1)} %compare_select_fusion, bf16[4096,256]{1,0:T(8,128)(2,1)} %multiply_convert_fusion, bf16[]{:T(256)} %constant.26.clone.1), kind=kCustom, calls=%fused_computation.29 | custom fusion | bytes 3146240 | tf_op jit(solution)/shard_map/scatter | solution.py:76
  70.5 2.5 %convolution_convert_fusion = bf16[169,6144]{1,0:T(8,128)(2,1)} fusion(bf16[169,256]{1,0:T(8,128)(2,1)S(1)} %gather_fusion, bf16[6144,256]{1,0:T(8,128)(2,1)S(1)} %scatter_custom_fusion), kind=kOutput, calls=%fused_computation.5 | convolution fusion | flops 532666368 | bytes 5308928 | tf_op jit(solution)/shard_map/dot_general | solution.py:77
  73.1 5.9 %reshape.27 = bf16[169,3,2048]{2,1,0:T(4,128)(2,1)S(1)} reshape(bf16[169,6144]{1,0:T(8,128)(2,1)} %convolution_convert_fusion) | data formatting | bytes 4153344 | tf_op jit(solution)/shard_map/reshape | solution.py:80
  79.0 7.5 %copy.29 = bf16[169,3,2048]{0,1,2:T(4,128)(2,1)} copy(bf16[169,3,2048]{2,1,0:T(4,128)(2,1)S(1)} %reshape.27) | data formatting | bytes 4153344 | tf_op jit(solution)/shard_map/reshape | solution.py:80
  86.5 7.9 %reshape.48 = bf16[32,2,16224]{2,1,0:T(2,128)(2,1)S(1)} reshape(bf16[2048,3,169]{2,1,0:T(4,128)(2,1)} %bitcast.28) | data formatting | bytes 4153344
  94.4 50.9 %all_to_all.10 = bf16[32,2,16224]{2,1,0:T(2,128)(2,1)} all-to-all(bf16[32,2,16224]{2,1,0:T(2,128)(2,1)S(1)} %reshape.48), channel_id=1, replica_groups=mesh['strip'=8,'cell'=32] {'cell'}, dimensions={0} | all-to-all | bytes 4153344 | tf_op jit(solution)/shard_map/all_to_all | solution.py:81
  145.3 10.3 %reshape.49 = bf16[2048,3,169]{2,1,0:T(4,128)(2,1)} reshape(bf16[32,2,16224]{2,1,0:T(2,128)(2,1)} %all_to_all.10) | data formatting | bytes 4153344
  155.6 11.0 %fusion.30 = (bf16[169,1,2048]{0,1,2:T(2,128)(2,1)}, bf16[169,1,2048]{0,1,2:T(2,128)(2,1)S(1)}, bf16[169,1,2048]{0,1,2:T(2,128)(2,1)}) fusion(bf16[169,3,2048]{0,1,2:T(4,128)(2,1)} %bitcast.27), kind=kLoop, calls=%fused_computation.48 | loop fusion | bytes 4153344 | tf_op jit(solution)/shard_map/slice | solution.py:84
  166.6 5.8 %copy.34 = bf16[169,1,2048]{2,0,1:T(8,128)(2,1)} copy(bf16[169,1,2048]{0,1,2:T(2,128)(2,1)} %get-tuple-element.2) | data formatting | bytes 1384448
  172.4 5.7 %copy.36 = bf16[169,1,2048]{2,0,1:T(8,128)(2,1)} copy(bf16[169,1,2048]{0,1,2:T(2,128)(2,1)} %get-tuple-element.4) | data formatting | bytes 1384448
  178.1 13.8 %collective-permute-start.3 = (bf16[169,2048]{1,0:T(8,128)(2,1)}, bf16[169,2048]{1,0:T(8,128)(2,1)}, u32[]{:S(2)}, u32[]{:S(2)}) collective-permute-start(bf16[169,2048]{1,0:T(8,128)(2,1)} %bitcast.5), channel_id=1, source_target_pairs={{0,32},{32,64},{64,96},{96,128},{128,160},{160,192},{192,224},{224... | collective-permute-start | bytes 2076680 | tf_op jit(solution)/shard_map/ppermute | solution.py:12
  191.9 3.5 %fusion.7 = bf16[169,4096]{1,0:T(8,128)(2,1)} fusion(bf16[4096,256]{1,0:T(8,128)(2,1)} %multiply_convert_fusion, bf16[256,169]{0,1:T(8,128)(2,1)S(1)} %copy-done.1), kind=kOutput, calls=%fused_computation.14 | convolution fusion | flops 355110912 | bytes 3568128 | tf_op jit(solution)/shard_map/dot_general | solution.py:68
  196.7 3.8 %collective-permute-done.3 = bf16[169,2048]{1,0:T(8,128)(2,1)} collective-permute-done((bf16[169,2048]{1,0:T(8,128)(2,1)}, bf16[169,2048]{1,0:T(8,128)(2,1)}, u32[]{:S(2)}, u32[]{:S(2)}) %collective-permute-start.3) | collective-permute-done | bytes 692256 | tf_op jit(solution)/shard_map/ppermute | solution.py:12
  200.4 2.5 %collective-permute-done.2 = bf16[169,2048]{1,0:T(8,128)(2,1)} collective-permute-done((bf16[169,2048]{1,0:T(8,128)(2,1)}, bf16[169,2048]{1,0:T(8,128)(2,1)}, u32[]{:S(2)}, u32[]{:S(2)}) %collective-permute-start.2) | collective-permute-done | bytes 692256 | tf_op jit(solution)/shard_map/ppermute | solution.py:12
  204.5 1.8 copy.33
  207.8 3.2 %copy.37 = bf16[22,8,3,2048]{3,1,2,0:T(8,128)(2,1)} copy(bf16[22,8,3,2048]{3,2,1,0:T(4,128)(2,1)S(1)} %bitcast.29) | data formatting | bytes 4325376
  (34 shorter events, 9.6 us)
Async XLA Ops:
  0.6 0.9 copy-start
  2.6 6.5 %collective-permute-start.1 = (bf16[256,256]{1,0:T(8,128)(2,1)S(1)}, bf16[256,256]{1,0:T(8,128)(2,1)S(1)}, u32[]{:S(2)}, u32[]{:S(2)}) collective-permute-start(bf16[256,256]{1,0:T(8,128)(2,1)S(1)} %convolution_convert_fusion.3), channel_id=1, source_target_pairs={{0,224},{32,0},{64,32},{96,64},{128,96},{160,128},{192,160},{224,1... | collective-permute-start | bytes 393224 | tf_op jit(solution)/shard_map/ppermute | solution.py:12
  5.8 3.3 %collective-permute-start = (bf16[256,256]{1,0:T(8,128)(2,1)S(1)}, bf16[256,256]{1,0:T(8,128)(2,1)S(1)}, u32[]{:S(2)}, u32[]{:S(2)}) collective-permute-start(bf16[256,256]{1,0:T(8,128)(2,1)S(1)} %convolution_convert_fusion.3), channel_id=1, source_target_pairs={{0,32},{32,64},{64,96},{96,128},{128,160},{160,192},{192,224},{224... | collective-permute-start | bytes 393224 | tf_op jit(solution)/shard_map/ppermute | solution.py:12
  9.1 12.7 %copy-start.4 = (s32[4096]{0:T(1024)S(1)}, s32[4096]{0:T(1024)}, u32[]{:S(2)}) copy-start(s32[4096]{0:T(1024)} %param.17) | copy-start | bytes 49156
  9.1 12.7 %copy-start.5 = (f32[4096]{0:T(1024)S(1)}, f32[4096]{0:T(1024)}, u32[]{:S(2)}) copy-start(f32[4096]{0:T(1024)} %param.18) | copy-start | bytes 49156
  9.1 12.7 %copy-start.2 = (bf16[256,256]{1,0:T(8,128)(2,1)S(1)}, bf16[256,256]{1,0:T(8,128)(2,1)}, u32[]{:S(2)}) copy-start(bf16[256,256]{1,0:T(8,128)(2,1)} %param.20) | copy-start | bytes 393220
  9.1 12.7 %copy-start.3 = (s32[4096]{0:T(1024)S(1)}, s32[4096]{0:T(1024)}, u32[]{:S(2)}) copy-start(s32[4096]{0:T(1024)} %param.15) | copy-start | bytes 49156
  11.0 13.7 %copy-start.8 = (bf16[128,256]{1,0:T(8,128)(2,1)S(1)}, bf16[128,256]{1,0:T(8,128)(2,1)}, u32[]{:S(2)}) copy-start(bf16[128,256]{1,0:T(8,128)(2,1)} %param.22) | copy-start | bytes 196612
  11.0 26.7 %all-to-all-start = ((bf16[32,48,256]{2,1,0:T(8,128)(2,1)}), bf16[32,48,256]{2,1,0:T(8,128)(2,1)S(1)}, u32[]{:S(2)}, u32[]{:S(2)}) async-start(bf16[32,48,256]{2,1,0:T(8,128)(2,1)} %bitcast), calls=%async_computation | async-start | bytes 1572864 | tf_op jit(solution)/shard_map/all_to_all | solution.py:52
  24.7 13.0 %copy-start.9 = (s32[4096]{0:T(1024)S(1)}, s32[4096]{0:T(1024)}, u32[]{:S(2)}) copy-start(s32[4096]{0:T(1024)} %param.16) | copy-start | bytes 49156
  37.7 7.8 %copy-start.6 = (bf16[256,256]{1,0:T(8,128)(2,1)S(1)}, bf16[256,256]{1,0:T(8,128)(2,1)}, u32[]{:S(2)}) copy-start(bf16[256,256]{1,0:T(8,128)(2,1)} %param.24) | copy-start | bytes 393220
  37.7 7.8 %copy-start.7 = (bf16[256,256]{1,0:T(8,128)(2,1)S(1)}, bf16[256,256]{1,0:T(8,128)(2,1)}, u32[]{:S(2)}) copy-start(bf16[256,256]{1,0:T(8,128)(2,1)} %param.23) | copy-start | bytes 393220
  166.6 25.3 %copy-start.1 = (bf16[256,169]{0,1:T(8,128)(2,1)S(1)}, bf16[256,169]{0,1:T(8,128)(2,1)}, u32[]{:S(2)}) copy-start(bf16[256,169]{0,1:T(8,128)(2,1)} %param.25) | copy-start | bytes 259588
  178.1 22.3 %collective-permute-start.3 = (bf16[169,2048]{1,0:T(8,128)(2,1)}, bf16[169,2048]{1,0:T(8,128)(2,1)}, u32[]{:S(2)}, u32[]{:S(2)}) collective-permute-start(bf16[169,2048]{1,0:T(8,128)(2,1)} %bitcast.5), channel_id=1, source_target_pairs={{0,32},{32,64},{64,96},{96,128},{128,160},{160,192},{192,224},{224... | collective-permute-start | bytes 2076680 | tf_op jit(solution)/shard_map/ppermute | solution.py:12
  191.9 11.0 %collective-permute-start.2 = (bf16[169,2048]{1,0:T(8,128)(2,1)}, bf16[169,2048]{1,0:T(8,128)(2,1)}, u32[]{:S(2)}, u32[]{:S(2)}) collective-permute-start(bf16[169,2048]{1,0:T(8,128)(2,1)} %bitcast.3), channel_id=1, source_target_pairs={{0,224},{32,0},{64,32},{96,64},{128,96},{160,128},{192,160},{224,1... | collective-permute-start | bytes 2076680 | tf_op jit(solution)/shard_map/ppermute | solution.py:12

commit v2 on v1

v2 whole, which is shorter than its diff:
```python
import functools

import jax
import jax.numpy as jnp
import numpy as np
from jax import lax
from jax.experimental import pallas as pl
from jax.experimental.pallas import tpu as pltpu
from jax.sharding import PartitionSpec as P

MESH = pl.DeviceIdType.MESH
F32 = jnp.float32
BF16 = jnp.bfloat16
D = 256
BLOCK = 169
ORB = 13
HALF = 88
FETCH = 48
SLOT = 64
CELLS = 32
STRIPS = 8
Z = 8
X = 4
PAIRS = 4096
GROUPS = 96
CUTOFF = 8.0
COUNT = 128


def silu(x):
    half = 0.5 * x
    return half + half * jnp.tanh(half)


def offset_of(k):
    j = lax.div(k, 4)
    hop = lax.div(j + 1, 2) * (2 * lax.rem(j, 2) - 1)
    return lax.rem(k, 4), hop


def cell_at(k, sign):
    c = lax.axis_index("cell")
    dx, dz = offset_of(k)
    x = lax.rem(lax.div(c, Z) + sign * dx + X, X)
    z = lax.rem(lax.rem(c, Z) + sign * dz + Z, Z)
    return x * Z + z


def strip_at(step):
    return lax.rem(lax.axis_index("strip") + step + STRIPS, STRIPS)


def column(values, lane):
    lanes = lax.broadcasted_iota(jnp.int32, values.shape, 1)
    return jnp.sum(jnp.where(lanes == lane, values, 0.0), axis=1, keepdims=True)


def one_hot(index, width):
    lanes = lax.broadcasted_iota(jnp.int32, (index.shape[0], width), 1)
    return jnp.where(lanes == index.astype(jnp.int32), 1.0, 0.0).astype(BF16)


def dot(a, b):
    return jnp.dot(a, b, preferred_element_type=F32)


def dot_nt(a, b):
    return lax.dot_general(a, b, (((1,), (1,)), ((), ())), preferred_element_type=F32)


def envelope_of(distance):
    return 0.5 * (jnp.cos(jnp.pi * distance / CUTOFF) + 1.0)


def gate_of(distance, envelope, w_in, w_out):
    centers = lax.broadcasted_iota(jnp.int32, (1, COUNT), 1).astype(F32) * (CUTOFF / (COUNT - 1))
    scaled = (distance - centers) * (COUNT / (2.0 * CUTOFF))
    basis = (jnp.exp(-scaled * scaled) * envelope).astype(BF16)
    radial = silu(dot(basis, w_in)).astype(BF16)
    return dot(radial, w_out)


def main_kernel(
    feat, atom, prow, slot, dist, lists, w_left, w_right, w_rin, w_rout, w_mix, w_out,
    own, blk_in,
    feat_in, tables, left, rows_out, rows_in, gate_s, gate_o, blk_out,
    slot_d, slot_e, slot_a, slot_m, pair_d, pair_e, pair_a, pair_r, list_t,
    square, w_pad, w_own, w_flip,
    feat_ss, feat_rs, rows_ss, rows_rs, blk_ss, blk_rs, local_sem,
):
    me = lax.axis_index("cell")
    barrier = pltpu.get_barrier_semaphore()

    def greet(k, _):
        c = cell_at(k, 1)
        for step in (-1, 0, 1):
            if step:
                pl.semaphore_signal(barrier, inc=1, device_id=(strip_at(step), c), device_id_type=MESH)
            else:
                @pl.when(k > 0)
                def _():
                    pl.semaphore_signal(barrier, inc=1, device_id=(strip_at(0), c), device_id_type=MESH)
        return 0

    lax.fori_loop(0, CELLS, greet, 0)

    left[...] = dot(feat[...], w_left[...]).astype(BF16)
    tables[pl.ds(D, D), :] = dot(feat[...], w_right[...]).astype(BF16)

    w_pad[...] = jnp.zeros_like(w_pad)
    w_pad[:, 0:BLOCK] = w_out[...]
    entry = lax.broadcasted_iota(jnp.int32, (2 * HALF, D), 0)
    lane = lax.broadcasted_iota(jnp.int32, (2 * HALF, D), 1)
    quotient = lax.shift_right_logical(entry * 79, 10)
    flipped = (entry - quotient * ORB) * ORB + quotient
    keep = entry < BLOCK
    w_own[...] = dot_nt(jnp.where(keep & (lane == entry), 1.0, 0.0).astype(BF16), w_pad[...]).astype(BF16)
    w_flip[...] = dot_nt(jnp.where(keep & (lane == flipped), 1.0, 0.0).astype(BF16), w_pad[...]).astype(BF16)

    def place(j, total):
        left_parts, right_parts = [], []
        for h in range(2):
            at = pl.ds(2 * j + h, 1)
            t = slot[at, :]
            d = dist[at, :]
            d_hi = d.astype(BF16).astype(F32)
            d_mid = (d - d_hi).astype(BF16).astype(F32)
            d_lo = d - d_hi - d_mid
            k = prow[at, :] - FETCH * (lax.shift_right_logical(t, 6) & (CELLS - 1))
            hit = lax.broadcasted_iota(jnp.int32, (SLOT, 128), 0) == (t & (SLOT - 1))
            parts = (d_hi, d_mid, d_lo, (atom[at, :] + 1).astype(F32), k.astype(F32))
            left_parts.append(jnp.concatenate([jnp.where(hit, v, 0.0) for v in parts], axis=0))
            group = lax.broadcasted_iota(jnp.int32, (128, 128), 0) == lax.shift_right_logical(t, 6)
            right_parts.append(jnp.where(group, 1.0, 0.0))
        return total + dot_nt(
            jnp.concatenate(left_parts, axis=1).astype(BF16), jnp.concatenate(right_parts, axis=1).astype(BF16)
        )

    total = lax.fori_loop(0, PAIRS // 256, place, jnp.zeros((5 * SLOT, 128), F32))
    d = total[0:SLOT] + total[SLOT:2 * SLOT] + total[2 * SLOT:3 * SLOT]
    slot_d[...] = d
    slot_e[...] = envelope_of(d)
    slot_a[...] = total[3 * SLOT:4 * SLOT] - 1.0
    slot_m[...] = total[4 * SLOT:5 * SLOT]

    square[...] = jnp.zeros_like(square)
    for source, target in ((dist[...], pair_d), (envelope_of(dist[...]), pair_e), (atom[...].astype(F32), pair_a), (prow[...].astype(F32), pair_r)):
        square[0:32, :] = source
        target[...] = square[...].T
    square[0:32, 0:FETCH] = lists[...].astype(F32)
    list_t[...] = square[...].T

    pl.semaphore_wait(barrier, 3 * CELLS - 1)

    def feature_copy(which):
        return pltpu.make_async_remote_copy(
            src_ref=feat, dst_ref=feat_in.at[which], send_sem=feat_ss.at[which], recv_sem=feat_rs.at[which],
            device_id=(strip_at(1 - 2 * which), me), device_id_type=MESH,
        )

    for which in range(2):
        feature_copy(which).start()

    def pair_gates(j, _):
        d = jnp.concatenate([column(pair_d[...], 2 * j + h) for h in range(2)], axis=0)
        e = jnp.concatenate([column(pair_e[...], 2 * j + h) for h in range(2)], axis=0)
        gate_o[pl.ds(pl.multiple_of(j * 256, 256), 256), :] = gate_of(d, e, w_rin[...], w_rout[...])
        return 0

    early = 4
    lax.fori_loop(0, early, pair_gates, 0)

    for which in range(2):
        feature_copy(which).wait()
        tables[pl.ds(2 * D * which, D), :] = dot(feat_in[which], w_right[...]).astype(BF16)

    def row_copy(k):
        return pltpu.make_async_remote_copy(
            src_ref=rows_out.at[pl.ds(pl.multiple_of(k * FETCH, 16), FETCH)],
            dst_ref=rows_in.at[pl.ds(pl.multiple_of(me * FETCH, 16), FETCH)],
            send_sem=rows_ss.at[k], recv_sem=rows_rs.at[k],
            device_id=(strip_at(0), cell_at(k, 1)), device_id_type=MESH,
        )

    own_rows = pltpu.make_async_copy(
        rows_out.at[pl.ds(0, FETCH)], rows_in.at[pl.ds(pl.multiple_of(me * FETCH, 16), FETCH)], local_sem.at[0]
    )

    def send_rows_of(i):
        for h in range(4):
            if h:
                row_copy(4 * i + h).start()
            else:
                @pl.when(i == 0)
                def _():
                    own_rows.start()

                @pl.when(i > 0)
                def _():
                    row_copy(4 * i).start()

    def pick(i, _):
        index = jnp.concatenate([column(list_t[0:FETCH, :], cell_at(4 * i + h, 1)) for h in range(4)], axis=0)
        picked = dot(one_hot(index, 3 * D), tables[...]).astype(BF16)
        rows_out[pl.ds(pl.multiple_of(i * 4 * FETCH, 64), 4 * FETCH), :] = picked

        @pl.when(i > 0)
        def _():
            send_rows_of(i - 1)
        return 0

    lax.fori_loop(0, CELLS // 4, pick, 0)

    def slot_columns(source, i):
        cells = [cell_at(2 * i + h, -1) for h in range(2)]
        return jnp.concatenate([column(source[...], o * CELLS + c) for o in range(3) for c in cells], axis=0)

    def slot_gates(i, _):
        gate_s[pl.ds(pl.multiple_of(i * 384, 128), 384), :] = gate_of(
            slot_columns(slot_d, i), slot_columns(slot_e, i), w_rin[...], w_rout[...]
        )
        return 0

    lax.fori_loop(0, 1, slot_gates, 0)
    send_rows_of(CELLS // 4 - 1)
    lax.fori_loop(1, CELLS // 2, slot_gates, 0)

    def block_copy(k, o):
        return pltpu.make_async_remote_copy(
            src_ref=blk_out.at[k, o], dst_ref=blk_in.at[o * CELLS + me],
            send_sem=blk_ss.at[k, o], recv_sem=blk_rs.at[k, o],
            device_id=(strip_at(o - 1), cell_at(k, -1)), device_id_type=MESH,
        )

    own_block = pltpu.make_async_copy(blk_out.at[0, 1], blk_in.at[CELLS + me], local_sem.at[1])

    def send_blocks_of(i):
        for h in range(2):
            for o in range(3):
                if h or o != 1:
                    block_copy(2 * i + h, o).start()
                else:
                    @pl.when(i == 0)
                    def _():
                        own_block.start()

                    @pl.when(i > 0)
                    def _():
                        block_copy(2 * i, 1).start()

    def slots(i, _):
        @pl.when(i == 0)
        def _():
            own_rows.wait()

        @pl.when(i > 0)
        def _():
            row_copy(2 * i).wait_recv()
        row_copy(2 * i + 1).wait_recv()
        rows = jnp.concatenate(
            [rows_in[pl.ds(pl.multiple_of(cell_at(2 * i + h, -1) * FETCH, 16), FETCH), :] for h in range(2)], axis=0
        )
        second = lax.rem(lax.div(lax.broadcasted_iota(jnp.int32, (384, 1), 0), SLOT), 2) * FETCH
        left_rows = dot(one_hot(slot_columns(slot_a, i), D), left[...])
        right_rows = dot(one_hot(slot_columns(slot_m, i).astype(jnp.int32) + second, 2 * FETCH), rows)
        gate = gate_s[pl.ds(pl.multiple_of(i * 384, 128), 384), :]
        edge = (left_rows * right_rows * gate).astype(BF16)
        mixed = silu(dot(edge, w_mix[...])).astype(BF16)
        out = dot_nt(w_flip[...], mixed)
        low = lax.broadcasted_iota(jnp.int32, (HALF, 128), 1) < SLOT
        for o in range(3):
            top = out[0:HALF, o * 128:(o + 1) * 128]
            bottom = out[HALF:2 * HALF, o * 128:(o + 1) * 128]
            blk_out[2 * i, o] = jnp.where(low, top, pltpu.roll(bottom, SLOT, 1)).astype(BF16)
            blk_out[2 * i + 1, o] = jnp.where(low, pltpu.roll(top, SLOT, 1), bottom).astype(BF16)

        @pl.when(i > 0)
        def _():
            send_blocks_of(i - 1)
        return 0

    lax.fori_loop(0, CELLS // 2, slots, 0)
    lax.fori_loop(early, early + 1, pair_gates, 0)
    send_blocks_of(CELLS // 2 - 1)
    lax.fori_loop(early + 1, PAIRS // 256, pair_gates, 0)

    def pairs(j, _):
        index_l = jnp.concatenate([column(pair_a[...], 2 * j + h) for h in range(2)], axis=0)
        index_r = jnp.concatenate([column(pair_r[...], 2 * j + h) for h in range(2)], axis=0)
        left_rows = dot(one_hot(index_l, D), left[...])
        right_rows = dot(one_hot(index_r, CELLS * FETCH), rows_in[...])
        at = pl.ds(pl.multiple_of(j * 256, 256), 256)
        edge = (left_rows * right_rows * gate_o[at, :]).astype(BF16)
        mixed = silu(dot(edge, w_mix[...])).astype(BF16)
        own[:, at] = dot_nt(w_own[...], mixed)[0:BLOCK].astype(BF16)
        return 0

    lax.fori_loop(0, PAIRS // 256, pairs, 0)

    own_block.wait()
    block_copy(0, 0).wait()
    block_copy(0, 2).wait()

    def finish(k, _):
        row_copy(k).wait_send()
        for o in range(3):
            block_copy(k, o).wait()
        return 0

    lax.fori_loop(1, CELLS, finish, 0)


STEPS = 8


def unpack_kernel(own_in, blocks, own, partner):
    own[...] = own_in[...]
    low = lax.broadcasted_iota(jnp.int32, (HALF, 128), 1) < SLOT
    for q in range(GROUPS // STEPS // 2):
        even = blocks[2 * q].astype(F32)
        odd = blocks[2 * q + 1].astype(F32)
        top = jnp.where(low, even, pltpu.roll(odd, SLOT, 1))
        bottom = jnp.where(low, pltpu.roll(even, SLOT, 1), odd)
        partner[:, q * 128:(q + 1) * 128] = jnp.concatenate([top, bottom], axis=0)[0:BLOCK].astype(BF16)


def body(features, pair_atom, partner_row, transpose_slot, distance, send_rows, w_left, w_right, w_radial_in, w_radial_out, w_mix, w_out):
    vmem = pl.BlockSpec(memory_space=pltpu.VMEM)
    sem = pltpu.SemaphoreType.DMA
    own, blocks = pl.pallas_call(
        main_kernel,
        out_shape=(
            jax.ShapeDtypeStruct((BLOCK, PAIRS), BF16),
            jax.ShapeDtypeStruct((GROUPS, HALF, 128), BF16),
        ),
        in_specs=[vmem] * 12,
        out_specs=(vmem, pl.BlockSpec(memory_space=pl.ANY)),
        scratch_shapes=[
            pltpu.VMEM((2, D, D), BF16),
            pltpu.VMEM((3 * D, D), BF16),
            pltpu.VMEM((D, D), BF16),
            pltpu.VMEM((CELLS * FETCH, D), BF16),
            pltpu.VMEM((CELLS * FETCH, D), BF16),
            pltpu.VMEM((GROUPS * SLOT, D), F32),
            pltpu.VMEM((PAIRS, D), F32),
            pltpu.VMEM((CELLS, 3, HALF, 128), BF16),
            *[pltpu.VMEM((SLOT, 128), F32)] * 4,
            *[pltpu.VMEM((128, 128), F32)] * 5,
            pltpu.VMEM((128, 128), F32),
            pltpu.VMEM((D, D), BF16),
            pltpu.VMEM((2 * HALF, D), BF16),
            pltpu.VMEM((2 * HALF, D), BF16),
            sem((2,)), sem((2,)), sem((CELLS,)), sem((CELLS,)), sem((CELLS, 3)), sem((CELLS, 3)), sem((2,)),
        ],
        compiler_params=pltpu.CompilerParams(collective_id=0, has_side_effects=True, vmem_limit_bytes=48 << 20),
    )(
        features,
        pair_atom.reshape(32, 128),
        partner_row.reshape(32, 128),
        transpose_slot.reshape(32, 128),
        distance.reshape(32, 128),
        send_rows, w_left, w_right, w_radial_in, w_radial_out, w_mix, w_out,
    )
    own_width, partner_width = PAIRS // STEPS, GROUPS * SLOT // STEPS
    return pl.pallas_call(
        unpack_kernel,
        grid=(STEPS,),
        out_shape=(
            jax.ShapeDtypeStruct((BLOCK, PAIRS), BF16),
            jax.ShapeDtypeStruct((BLOCK, GROUPS * SLOT), BF16),
        ),
        in_specs=[
            pl.BlockSpec((BLOCK, own_width), lambda i: (0, i)),
            pl.BlockSpec((GROUPS // STEPS, HALF, 128), lambda i: (i, 0, 0)),
        ],
        out_specs=(
            pl.BlockSpec((BLOCK, own_width), lambda i: (0, i)),
            pl.BlockSpec((BLOCK, partner_width), lambda i: (0, i)),
        ),
        compiler_params=pltpu.CompilerParams(vmem_limit_bytes=16 << 20),
    )(own, blocks)


def solution(mesh):
    both = P(("strip", "cell"))
    rows = P(("strip", "cell"), None)
    in_specs = (rows, both, both, both, both, rows, P(), P(), P(), P(), P(), P())
    out_specs = (P(None, ("strip", "cell")), P(None, ("strip", "cell")))
    return jax.shard_map(body, mesh=mesh, in_specs=in_specs, out_specs=out_specs, check_vma=False)
```

time: 212 us -> 107 us (0.50)
  Pallas kernels: 0 us -> 94.4 us
  local copies, waits for them, and re-layouts: 84.7 us -> 9.93 us
  blocking collectives: 50.9 us -> 0 us
  matrix products: 29.7 us -> 0 us
  starting transfers between devices: 27.7 us -> 0 us
  waiting for transfers between devices: 14.8 us -> 0 us
  other arithmetic: 2.34 us -> 0 us
    pallas_call x0 -> x2, Pallas kernels: none -> 94.4 us  [the longest x1 90.7 us: body(): pl.pallas_call(main_kernel, out_shape=(jax.ShapeDtypeStruct((BLOCK, PAIRS...]
    all_to_all x1 -> x0, blocking collectives: 50.9 us -> none  [body(): lax.all_to_all(outbox, 'cell', split_axis=2, concat_axis=2, tiled=True)]
    dot_general x8 -> x0, matrix products: 29.7 us -> none  [the longest x3 12.6 us: select_rows(): jnp.dot(picker, table, preferred_element_type=jnp.float32)]
    unnamed x27 -> x23, local copies, waits for them, and re-layouts: 36.5 us -> 9.93 us
    scatter x1 -> x0, local copies, waits for them, and re-layouts: 19.5 us -> none  [body(): jnp.zeros((slot_total, width), jnp.bfloat16).at[transpose_slot].set(mixed)]
    ppermute x4 -> x0, starting transfers between devices: 17 us -> none  [passed_along(): return lax.ppermute(x, axis, [(i, (i + by) % peers) for i in range(peers)])]
    reshape x2 -> x0, local copies, waits for them, and re-layouts: 13.5 us -> none  [body(): outbox = outbox.reshape(entries, 3, slot_total // 3)]
    slice x1 -> x0, local copies, waits for them, and re-layouts: 11 us -> none  [body(): pieces[which] = passed_along(arrived[:, which], 'strip', offset)]
  transfers between devices with their start and end apart: 5 -> 0, of which waited for: 3 -> 0; matrix products, arithmetic and copies ran while one was open for 7% -> 0% of each run, Pallas kernels for 0% -> 0%
where the time goes in v2:
time: 107 us; the launch traced here: 105 us
  Pallas kernels  94.4 us (88%)
  local copies, waits for them, and re-layouts  9.93 us (9%)
    pallas_call x1, Pallas kernels, body(): pl.pallas_call(main_kernel, out_shape=(jax.ShapeDtypeStruct((BLOCK, PAIRS...  90.7 us
    unnamed x23, local copies, waits for them, and re-layouts  9.93 us
    pallas_call x1, Pallas kernels, body(): pl.pallas_call(unpack_kernel, grid=(STEPS,), out_shape=(jax.ShapeDtypeStr...  3.68 us

profile of v2, /device:TPU:1, one launch (start us, length us, event | category | flops | bytes accessed | tf_op | source)
XLA Modules:
  0.0 104.9 jit_solution(2805542851529195003)
XLA Ops:
  0.6 1.0 copy.14.w_out
  1.6 0.0 copy-start
  1.6 0.9 copy-done
  2.5 0.0 copy-start.1
  2.5 0.9 copy-done.1
  3.4 0.0 copy-start.2
  3.4 0.9 copy-done.2
  4.3 0.0 copy-start.3
  4.3 0.9 copy-done.3
  5.2 0.0 copy-start.4
  5.2 0.9 copy-done.4
  6.2 0.0 copy-start.5
  6.2 0.8 copy-done.5
  7.0 0.0 copy-start.6
  7.0 0.7 copy-done.6
  7.7 0.0 copy-start.7
  7.7 0.7 copy-done.7
  8.4 0.0 copy-start.8
  8.4 0.7 copy-done.8
  9.1 0.0 copy-start.9
  9.1 0.7 copy-done.9
  9.9 0.7 copy-done.10
  10.6 90.7 %shard_map.131 = (bf16[169,4096]{1,0:T(8,128)(2,1)S(1)}, bf16[96,88,128]{2,1,0:T(8,128)(2,1)S(1)}) custom-call(bf16[256,256]{1,0:T(8,128)(2,1)S(1)} %copy-done, s32[32,128]{1,0:T(8,128)S(1)} %bitcast.4, s32[32,128]{1,0:T(8,128)S(1)} %bitcast.5, s32[32,128]{1,0:T(8,128)S(1)} %bitcast.6, f32[32,128]{1,0:T(8,128)S(1)} %bitcast.7, s32[32,48]{1,0:T(8,128)S(1)} %copy-done.10, ...), custom_call_target="tpu_custom_call" | custom-call | tf_op jit(solution)/shard_map/pallas_call | solution.py:330
  101.3 3.7 %shard_map.132 = (bf16[169,4096]{1,0:T(8,128)(2,1)}, bf16[169,6144]{1,0:T(8,128)(2,1)}) custom-call(bf16[169,4096]{1,0:T(8,128)(2,1)S(1)} %get-tuple-element.4.own_in, bf16[96,88,128]{2,1,0:T(8,128)(2,1)S(1)} %get-tuple-element.5.blocks), custom_call_target="tpu_custom_call" | custom-call | tf_op jit(solution)/shard_map/pallas_call | solution.py:365
  (1 shorter events, 0.0 us)
Async XLA Ops:
  1.6 0.9 copy-start
  2.5 0.9 copy-start.1
  3.4 0.9 copy-start.2
  4.3 0.9 copy-start.3
  5.2 0.9 copy-start.4
  6.2 0.8 copy-start.5
  7.0 0.7 copy-start.6
  7.7 0.7 copy-start.7
  8.4 0.7 copy-start.8
  9.1 0.7 copy-start.9
  9.9 0.7 copy-start.10

commit v3 on v2

v3 whole, which is shorter than its diff:
```python
import functools

import jax
import jax.numpy as jnp
import numpy as np
from jax import lax
from jax.experimental import pallas as pl
from jax.experimental.pallas import tpu as pltpu
from jax.sharding import PartitionSpec as P

MESH = pl.DeviceIdType.MESH
F32 = jnp.float32
BF16 = jnp.bfloat16
D = 256
BLOCK = 169
ORB = 13
HALF = 88
FETCH = 48
SLOT = 64
CELLS = 32
STRIPS = 8
Z = 8
X = 4
PAIRS = 4096
GROUPS = 96
CUTOFF = 8.0
COUNT = 128
PART = 16
EARLY = 4


def silu(x):
    half = 0.5 * x
    return half + half * jnp.tanh(half)


def offset_of(k):
    j = lax.div(k, 4)
    hop = lax.div(j + 1, 2) * (2 * lax.rem(j, 2) - 1)
    return lax.rem(k, 4), hop


def cell_at(k, sign):
    c = lax.axis_index("cell")
    dx, dz = offset_of(k)
    x = lax.rem(lax.div(c, Z) + sign * dx + X, X)
    z = lax.rem(lax.rem(c, Z) + sign * dz + Z, Z)
    return x * Z + z


def strip_at(step):
    return lax.rem(lax.axis_index("strip") + step + STRIPS, STRIPS)


def column(values, lane):
    lanes = lax.broadcasted_iota(jnp.int32, values.shape, 1)
    return jnp.sum(jnp.where(lanes == lane, values, 0.0), axis=1, keepdims=True)


def one_hot(index, width):
    lanes = lax.broadcasted_iota(jnp.int32, (index.shape[0], width), 1)
    return jnp.where(lanes == index.astype(jnp.int32), 1.0, 0.0).astype(BF16)


def dot(a, b):
    return jnp.dot(a, b, preferred_element_type=F32)


def dot_nt(a, b):
    return lax.dot_general(a, b, (((1,), (1,)), ((), ())), preferred_element_type=F32)


def row_index(slot, row):
    offset = lax.shift_right_logical(slot, 11)
    base = FETCH * (lax.shift_right_logical(slot, 6) & (CELLS - 1))
    part = lax.shift_right_logical((row - base - offset) * 171, 9)
    return base + offset * PART + part


def envelope_of(distance):
    return 0.5 * (jnp.cos(jnp.pi * distance / CUTOFF) + 1.0)


def gate_of(distance, envelope, w_in, w_out):
    centers = lax.broadcasted_iota(jnp.int32, (1, COUNT), 1).astype(F32) * (CUTOFF / (COUNT - 1))
    scaled = (distance - centers) * (COUNT / (2.0 * CUTOFF))
    basis = (jnp.exp(-scaled * scaled) * envelope).astype(BF16)
    radial = silu(dot(basis, w_in)).astype(BF16)
    return dot(radial, w_out)


def main_kernel(
    feat_h, atom_h, prow_h, slot_h, dist_h, lists_h, w_left_h, w_right_h, w_rin_h, w_rout_h, w_mix_h, w_out_h,
    own, partner,
    feat, atom, prow, slot, dist, lists, w_left, w_right, w_rin, w_rout, w_mix, w_raw, w_out,
    feat_in, tables, left, rows_out, rows_in, gate_s, gate_o, blk_out, blk_in,
    slot_d, slot_e, slot_a, slot_m, pair_d, pair_e, pair_a, pair_r, list_t, list_s,
    square, w_own, w_flip,
    in_sem, feat_ss, feat_rs, rows_ss, rows_rs, blk_ss, blk_rs, local_sem,
):
    me = lax.axis_index("cell")
    sources = (feat_h, w_left_h, w_right_h, lists_h, slot_h, dist_h, atom_h, prow_h, w_out_h, w_rin_h, w_rout_h, w_mix_h)
    targets = (feat, w_left, w_right, lists, slot, dist, atom, prow, w_raw, w_rin, w_rout, w_mix)
    loads = [pltpu.make_async_copy(a, b, in_sem.at[n]) for n, (a, b) in enumerate(zip(sources, targets))]
    for load in loads:
        load.start()

    barrier = pltpu.get_barrier_semaphore()

    def greet(k, _):
        c = cell_at(k, 1)
        for step in (-1, 0, 1):
            if step:
                pl.semaphore_signal(barrier, inc=1, device_id=(strip_at(step), c), device_id_type=MESH)
            else:
                @pl.when(k > 0)
                def _():
                    pl.semaphore_signal(barrier, inc=1, device_id=(strip_at(0), c), device_id_type=MESH)
        return 0

    lax.fori_loop(0, CELLS, greet, 0)
    for load in loads:
        load.wait()

    left[...] = dot(feat[...], w_left[...]).astype(BF16)
    tables[1] = dot(feat[...], w_right[...]).astype(BF16)

    square[...] = jnp.zeros_like(square)
    square[0:32, 0:FETCH] = lists[...].astype(F32)
    list_t[...] = square[...].T
    for o in range(3):
        list_s[pl.ds(o * PART, PART), :] = list_t[pl.ds(o, PART, stride=3), :] - float(o * D)

    def pick(o, i):
        index = jnp.concatenate(
            [column(list_s[pl.ds(pl.multiple_of(o * PART, PART), PART), :], cell_at(8 * i + h, 1)) for h in range(8)], axis=0
        )
        picked = dot(one_hot(index, D), tables[o]).astype(BF16)
        rows_out[o, pl.ds(pl.multiple_of(i * 8 * PART, 128), 8 * PART), :] = picked

    def pick_own(i, _):
        pick(1, i)
        return 0

    lax.fori_loop(0, CELLS // 8, pick_own, 0)

    def place(j, total):
        left_parts, right_parts = [], []
        for h in range(2):
            at = pl.ds(2 * j + h, 1)
            t = slot[at, :]
            d = dist[at, :]
            d_hi = d.astype(BF16).astype(F32)
            d_mid = (d - d_hi).astype(BF16).astype(F32)
            d_lo = d - d_hi - d_mid
            index = row_index(t, prow[at, :]) - FETCH * (lax.shift_right_logical(t, 6) & (CELLS - 1))
            hit = lax.broadcasted_iota(jnp.int32, (SLOT, 128), 0) == (t & (SLOT - 1))
            parts = (d_hi, d_mid, d_lo, (atom[at, :] + 1).astype(F32), index.astype(F32))
            left_parts.append(jnp.concatenate([jnp.where(hit, v, 0.0) for v in parts], axis=0))
            group = lax.broadcasted_iota(jnp.int32, (128, 128), 0) == lax.shift_right_logical(t, 6)
            right_parts.append(jnp.where(group, 1.0, 0.0))
        return total + dot_nt(
            jnp.concatenate(left_parts, axis=1).astype(BF16), jnp.concatenate(right_parts, axis=1).astype(BF16)
        )

    total = lax.fori_loop(0, PAIRS // 256, place, jnp.zeros((5 * SLOT, 128), F32))
    d = total[0:SLOT] + total[SLOT:2 * SLOT] + total[2 * SLOT:3 * SLOT]
    slot_d[...] = d
    slot_e[...] = envelope_of(d)
    slot_a[...] = total[3 * SLOT:4 * SLOT] - 1.0
    slot_m[...] = total[4 * SLOT:5 * SLOT]

    pl.semaphore_wait(barrier, 3 * CELLS - 1)

    def feature_copy(which):
        return pltpu.make_async_remote_copy(
            src_ref=feat, dst_ref=feat_in.at[which], send_sem=feat_ss.at[which], recv_sem=feat_rs.at[which],
            device_id=(strip_at(1 - 2 * which), me), device_id_type=MESH,
        )

    def row_copy(k, o, sender):
        return pltpu.make_async_remote_copy(
            src_ref=rows_out.at[o, pl.ds(pl.multiple_of(k * PART, PART), PART)],
            dst_ref=rows_in.at[pl.ds(pl.multiple_of(me * FETCH + o * PART, PART), PART)],
            send_sem=rows_ss.at[k, o], recv_sem=rows_rs.at[sender, o],
            device_id=(strip_at(0), cell_at(k, 1)), device_id_type=MESH,
        )

    def own_rows(o):
        return pltpu.make_async_copy(
            rows_out.at[o, pl.ds(0, PART)], rows_in.at[pl.ds(pl.multiple_of(me * FETCH + o * PART, PART), PART)], local_sem.at[o]
        )

    def send_rows_of(o, i):
        for h in range(8):
            if h:
                row_copy(8 * i + h, o, me).start()
            else:
                @pl.when(i == 0)
                def _():
                    own_rows(o).start()

                @pl.when(i > 0)
                def _():
                    row_copy(8 * i, o, me).start()

    for which in range(2):
        feature_copy(which).start()

    def send_own_part(i, _):
        send_rows_of(1, i)
        return 0

    lax.fori_loop(0, CELLS // 8, send_own_part, 0)

    def slot_columns(source, i):
        cells = [cell_at(2 * i + h, -1) for h in range(2)]
        return jnp.concatenate([column(source[...], o * CELLS + c) for o in range(3) for c in cells], axis=0)

    def slot_gates(i, _):
        gate_s[pl.ds(pl.multiple_of(i * 384, 128), 384), :] = gate_of(
            slot_columns(slot_d, i), slot_columns(slot_e, i), w_rin[...], w_rout[...]
        )
        return 0

    early = EARLY
    lax.fori_loop(0, early, slot_gates, 0)

    for which in range(2):
        feature_copy(which).wait()
        tables[2 * which] = dot(feat_in[which], w_right[...]).astype(BF16)

    def pick_rest(i, _):
        pick(2 * lax.div(i, 4), lax.rem(i, 4))

        @pl.when(i > 0)
        def _():
            send_rows_of(2 * lax.div(i - 1, 4), lax.rem(i - 1, 4))
        return 0

    lax.fori_loop(0, CELLS // 4, pick_rest, 0)
    lax.fori_loop(early, early + 1, slot_gates, 0)
    send_rows_of(2, CELLS // 8 - 1)
    lax.fori_loop(early + 1, CELLS // 2, slot_gates, 0)

    def block_copy(k, o, sender):
        return pltpu.make_async_remote_copy(
            src_ref=blk_out.at[k, o], dst_ref=blk_in.at[o * CELLS + me],
            send_sem=blk_ss.at[k, o], recv_sem=blk_rs.at[sender, o],
            device_id=(strip_at(o - 1), cell_at(k, -1)), device_id_type=MESH,
        )

    own_block = pltpu.make_async_copy(blk_out.at[0, 1], blk_in.at[CELLS + me], local_sem.at[3])

    def send_blocks_of(i):
        for h in range(2):
            for o in range(3):
                if h or o != 1:
                    block_copy(2 * i + h, o, me).start()
                else:
                    @pl.when(i == 0)
                    def _():
                        own_block.start()

                    @pl.when(i > 0)
                    def _():
                        block_copy(2 * i, 1, me).start()

    low = lax.broadcasted_iota(jnp.int32, (HALF, 128), 1) < SLOT

    def slots(i, _):
        cells = [cell_at(2 * i + h, -1) for h in range(2)]
        for o in range(3):
            @pl.when(i == 0)
            def _():
                own_rows(o).wait()

            @pl.when(i > 0)
            def _():
                row_copy(2 * i, o, cells[0]).wait_recv()
            row_copy(2 * i + 1, o, cells[1]).wait_recv()
        rows = jnp.concatenate([rows_in[pl.ds(pl.multiple_of(c * FETCH, PART), FETCH), :] for c in cells], axis=0)
        second = lax.rem(lax.div(lax.broadcasted_iota(jnp.int32, (384, 1), 0), SLOT), 2) * FETCH
        left_rows = dot(one_hot(slot_columns(slot_a, i), D), left[...])
        right_rows = dot(one_hot(slot_columns(slot_m, i).astype(jnp.int32) + second, 2 * FETCH), rows)
        gate = gate_s[pl.ds(pl.multiple_of(i * 384, 128), 384), :]
        edge = (left_rows * right_rows * gate).astype(BF16)
        mixed = silu(dot(edge, w_mix[...])).astype(BF16)
        out = dot_nt(w_flip[...], mixed)
        for o in range(3):
            top = out[0:HALF, o * 128:(o + 1) * 128]
            bottom = out[HALF:2 * HALF, o * 128:(o + 1) * 128]
            blk_out[2 * i, o] = jnp.where(low, top, pltpu.roll(bottom, SLOT, 1)).astype(BF16)
            blk_out[2 * i + 1, o] = jnp.where(low, pltpu.roll(top, SLOT, 1), bottom).astype(BF16)

        @pl.when(i > 0)
        def _():
            send_blocks_of(i - 1)
        return 0

    entry = lax.broadcasted_iota(jnp.int32, (2 * HALF, D), 0)
    lane = lax.broadcasted_iota(jnp.int32, (2 * HALF, D), 1)
    quotient = lax.shift_right_logical(entry * 79, 10)
    flipped = (entry - quotient * ORB) * ORB + quotient
    w_out[...] = jnp.zeros_like(w_out)
    w_out[0:BLOCK, :] = w_raw[...]
    w_own[...] = w_out[0:2 * HALF, :]
    w_flip[...] = dot(jnp.where((entry < BLOCK) & (lane == flipped), 1.0, 0.0).astype(BF16), w_out[...]).astype(BF16)

    lax.fori_loop(0, CELLS // 2, slots, 0)

    index = row_index(slot[...], prow[...])
    for source, target in ((dist[...], pair_d), (envelope_of(dist[...]), pair_e), (atom[...].astype(F32), pair_a), (index.astype(F32), pair_r)):
        square[0:32, :] = source
        target[...] = square[...].T
    send_blocks_of(CELLS // 2 - 1)

    def pair_gates(j, _):
        d = jnp.concatenate([column(pair_d[...], 2 * j + h) for h in range(2)], axis=0)
        e = jnp.concatenate([column(pair_e[...], 2 * j + h) for h in range(2)], axis=0)
        gate_o[pl.ds(pl.multiple_of(j * 256, 256), 256), :] = gate_of(d, e, w_rin[...], w_rout[...])
        return 0

    lax.fori_loop(0, PAIRS // 256, pair_gates, 0)

    def pairs(j, _):
        index_l = jnp.concatenate([column(pair_a[...], 2 * j + h) for h in range(2)], axis=0)
        index_r = jnp.concatenate([column(pair_r[...], 2 * j + h) for h in range(2)], axis=0)
        left_rows = dot(one_hot(index_l, D), left[...])
        right_rows = dot(one_hot(index_r, CELLS * FETCH), rows_in[...])
        at = pl.ds(pl.multiple_of(j * 256, 256), 256)
        edge = (left_rows * right_rows * gate_o[at, :]).astype(BF16)
        mixed = silu(dot(edge, w_mix[...])).astype(BF16)
        own[:, at] = dot_nt(w_own[...], mixed)[0:BLOCK].astype(BF16)
        return 0

    lax.fori_loop(0, PAIRS // 256, pairs, 0)

    own_block.wait()
    block_copy(0, 0, me).wait()
    block_copy(0, 2, me).wait()
    parity = lax.rem(me, 2)

    def unpack(n, _):
        o = lax.rem(n, 3)
        x = lax.rem(lax.div(n, 3) + lax.div(me, Z), X)
        rank = lax.div(n, 3 * X)
        middle = lax.div(rank + 2, 3) * (1 + 2 * lax.rem(rank + parity, 2))
        shift = middle * lax.div(3 - rank + 2, 3) + 2 * lax.div(rank, 3)
        shift = lax.rem(shift, 4)
        even = x * Z + 2 * lax.rem(lax.div(lax.rem(me, Z), 2) + shift, 4)
        for h in range(2):
            @pl.when(even + h != me)
            def _():
                block_copy(0, o, even + h).wait_recv()
        base = o * CELLS + even
        first = blk_in[base].astype(F32)
        second = blk_in[base + 1].astype(F32)
        top = jnp.where(low, first, pltpu.roll(second, SLOT, 1))
        bottom = jnp.where(low, pltpu.roll(first, SLOT, 1), second)
        partner[:, pl.ds(pl.multiple_of(base * SLOT, 128), 128)] = jnp.concatenate([top, bottom], axis=0)[0:BLOCK].astype(BF16)
        return 0

    lax.fori_loop(0, GROUPS // 2, unpack, 0)

    def finish(k, _):
        for o in range(3):
            row_copy(k, o, me).wait_send()
            block_copy(k, o, me).wait_send()
        return 0

    lax.fori_loop(1, CELLS, finish, 0)


def output_kernel(own_in, partner_in, own, partner, sem):
    copies = [pltpu.make_async_copy(own_in, own, sem.at[0]), pltpu.make_async_copy(partner_in, partner, sem.at[1])]
    for copy in copies:
        copy.start()
    for copy in copies:
        copy.wait()


def body(features, pair_atom, partner_row, transpose_slot, distance, send_rows, w_left, w_right, w_radial_in, w_radial_out, w_mix, w_out):
    vmem = pl.BlockSpec(memory_space=pltpu.VMEM)
    hbm = pl.BlockSpec(memory_space=pltpu.HBM)
    sem = pltpu.SemaphoreType.DMA
    outputs = (
        jax.ShapeDtypeStruct((BLOCK, PAIRS), BF16),
        jax.ShapeDtypeStruct((BLOCK, GROUPS * SLOT), BF16),
    )
    own, partner = pl.pallas_call(
        main_kernel,
        out_shape=outputs,
        in_specs=[hbm] * 12,
        out_specs=(vmem, vmem),
        scratch_shapes=[
            pltpu.VMEM((D, D), BF16),
            *[pltpu.VMEM((32, 128), jnp.int32)] * 3,
            pltpu.VMEM((32, 128), F32),
            pltpu.VMEM((CELLS, FETCH), jnp.int32),
            pltpu.VMEM((D, D), BF16),
            pltpu.VMEM((D, D), BF16),
            pltpu.VMEM((COUNT, D), BF16),
            pltpu.VMEM((D, D), BF16),
            pltpu.VMEM((D, D), BF16),
            pltpu.VMEM((BLOCK, D), BF16),
            pltpu.VMEM((D, D), BF16),
            pltpu.VMEM((2, D, D), BF16),
            pltpu.VMEM((3, D, D), BF16),
            pltpu.VMEM((D, D), BF16),
            pltpu.VMEM((3, CELLS * PART, D), BF16),
            pltpu.VMEM((CELLS * FETCH, D), BF16),
            pltpu.VMEM((GROUPS * SLOT, D), F32),
            pltpu.VMEM((PAIRS, D), F32),
            pltpu.VMEM((CELLS, 3, HALF, 128), BF16),
            pltpu.VMEM((GROUPS, HALF, 128), BF16),
            *[pltpu.VMEM((SLOT, 128), F32)] * 4,
            *[pltpu.VMEM((128, 128), F32)] * 5,
            pltpu.VMEM((FETCH, 128), F32),
            pltpu.VMEM((128, 128), F32),
            pltpu.VMEM((2 * HALF, D), BF16),
            pltpu.VMEM((2 * HALF, D), BF16),
            sem((12,)), sem((2,)), sem((2,)), sem((CELLS, 3)), sem((CELLS, 3)), sem((CELLS, 3)), sem((CELLS, 3)), sem((4,)),
        ],
        compiler_params=pltpu.CompilerParams(collective_id=0, has_side_effects=True, vmem_limit_bytes=48 << 20),
    )(*[pltpu.with_memory_space_constraint(a, pltpu.HBM) for a in (
        features,
        pair_atom.reshape(32, 128),
        partner_row.reshape(32, 128),
        transpose_slot.reshape(32, 128),
        distance.reshape(32, 128),
        send_rows, w_left, w_right, w_radial_in, w_radial_out, w_mix, w_out.T,
    )])
    return pl.pallas_call(
        output_kernel,
        out_shape=outputs,
        in_specs=[vmem, vmem],
        out_specs=(hbm, hbm),
        scratch_shapes=[sem((2,))],
        compiler_params=pltpu.CompilerParams(vmem_limit_bytes=16 << 20),
    )(own, partner)


def solution(mesh):
    both = P(("strip", "cell"))
    rows = P(("strip", "cell"), None)
    in_specs = (rows, both, both, both, both, rows, P(), P(), P(), P(), P(), P())
    out_specs = (P(None, ("strip", "cell")), P(None, ("strip", "cell")))
    return jax.shard_map(body, mesh=mesh, in_specs=in_specs, out_specs=out_specs, check_vma=False)
```

time: 107 us -> 92.2 us (0.86)
  the two profiles are of different devices: /device:TPU:1 before, /device:TPU:64 now
where the time goes in v3:
time: 92.2 us; the launch traced here: 92.1 us
  Pallas kernels  91.5 us (99%)
    pallas_call x1, Pallas kernels, body(): pl.pallas_call(main_kernel, out_shape=outputs, in_specs=[hbm] * 12, out_s...  89.6 us

profile of v3, /device:TPU:64, one launch (start us, length us, event | category | flops | bytes accessed | tf_op | source)
XLA Modules:
  0.0 92.1 jit_solution(13188859199767726107)
XLA Ops:
  0.6 89.6 %shard_map.131 = (bf16[169,4096]{1,0:T(8,128)(2,1)S(1)}, bf16[169,6144]{1,0:T(8,128)(2,1)S(1)}) custom-call(bf16[256,256]{1,0:T(8,128)(2,1)} %feat_h.1, s32[32,128]{1,0:T(8,128)} %bitcast.6, s32[32,128]{1,0:T(8,128)} %bitcast.7, s32[32,128]{1,0:T(8,128)} %bitcast.8, f32[32,128]{1,0:T(8,128)} %bitcast.9, s32[32,48]{1,0:T(8,128)} %lists_h.1, ...), custom_call_target="tpu_custom_call" | custom-call | tf_op jit(solution)/shard_map/pallas_call | solution.py:391
  90.3 1.8 %shard_map.132 = (bf16[169,4096]{1,0:T(8,128)(2,1)}, bf16[169,6144]{1,0:T(8,128)(2,1)}) custom-call(bf16[169,4096]{1,0:T(8,128)(2,1)S(1)} %get-tuple-element.4.own_in, bf16[169,6144]{1,0:T(8,128)(2,1)S(1)} %get-tuple-element.5.partner_in), custom_call_target="tpu_custom_call" | custom-call | tf_op jit(solution)/shard_map/pallas_call | solution.py:434

commit v4 on v3

--- a/solution.py
+++ b/solution.py
@@ -26,7 +26,9 @@
 CUTOFF = 8.0
 COUNT = 128
 PART = 16
-EARLY = 4
+EARLY = 2
+WIDE = 4
+SPAN = 3 * WIDE * SLOT
 
 
 def silu(x):
@@ -35,9 +37,9 @@
 
 
 def offset_of(k):
-    j = lax.div(k, 4)
+    j = lax.rem(k, Z)
     hop = lax.div(j + 1, 2) * (2 * lax.rem(j, 2) - 1)
-    return lax.rem(k, 4), hop
+    return lax.div(k, Z), hop
 
 
 def cell_at(k, sign):
@@ -58,8 +60,8 @@
 
 
 def one_hot(index, width):
-    lanes = lax.broadcasted_iota(jnp.int32, (index.shape[0], width), 1)
-    return jnp.where(lanes == index.astype(jnp.int32), 1.0, 0.0).astype(BF16)
+    lanes = lax.broadcasted_iota(jnp.int32, (index.shape[0], width), 1).astype(F32)
+    return jnp.where(lanes == index, 1.0, 0.0).astype(BF16)
 
 
 def dot(a, b):
@@ -214,11 +216,11 @@
     lax.fori_loop(0, CELLS // 8, send_own_part, 0)
 
     def slot_columns(source, i):
-        cells = [cell_at(2 * i + h, -1) for h in range(2)]
+        cells = [cell_at(WIDE * i + h, -1) for h in range(WIDE)]
         return jnp.concatenate([column(source[...], o * CELLS + c) for o in range(3) for c in cells], axis=0)
 
     def slot_gates(i, _):
-        gate_s[pl.ds(pl.multiple_of(i * 384, 128), 384), :] = gate_of(
+        gate_s[pl.ds(pl.multiple_of(i * SPAN, 128), SPAN), :] = gate_of(
             slot_columns(slot_d, i), slot_columns(slot_e, i), w_rin[...], w_rout[...]
         )
         return 0
@@ -241,7 +243,7 @@
     lax.fori_loop(0, CELLS // 4, pick_rest, 0)
     lax.fori_loop(early, early + 1, slot_gates, 0)
     send_rows_of(2, CELLS // 8 - 1)
-    lax.fori_loop(early + 1, CELLS // 2, slot_gates, 0)
+    lax.fori_loop(early + 1, CELLS // WIDE, slot_gates, 0)
 
     def block_copy(k, o, sender):
         return pltpu.make_async_remote_copy(
@@ -253,10 +255,10 @@
     own_block = pltpu.make_async_copy(blk_out.at[0, 1], blk_in.at[CELLS + me], local_sem.at[3])
 
     def send_blocks_of(i):
-        for h in range(2):
+        for h in range(WIDE):
             for o in range(3):
                 if h or o != 1:
-                    block_copy(2 * i + h, o, me).start()
+                    block_copy(WIDE * i + h, o, me).start()
                 else:
                     @pl.when(i == 0)
                     def _():
@@ -264,12 +266,12 @@
 
                     @pl.when(i > 0)
                     def _():
-                        block_copy(2 * i, 1, me).start()
+                        block_copy(WIDE * i, 1, me).start()
 
     low = lax.broadcasted_iota(jnp.int32, (HALF, 128), 1) < SLOT
 
     def slots(i, _):
-        cells = [cell_at(2 * i + h, -1) for h in range(2)]
+        cells = [cell_at(WIDE * i + h, -1) for h in range(WIDE)]
         for o in range(3):
             @pl.when(i == 0)
             def _():
@@ -277,21 +279,24 @@
 
             @pl.when(i > 0)
             def _():
-                row_copy(2 * i, o, cells[0]).wait_recv()
-            row_copy(2 * i + 1, o, cells[1]).wait_recv()
+                row_copy(WIDE * i, o, cells[0]).wait_recv()
+            for h in range(1, WIDE):
+                row_copy(WIDE * i + h, o, cells[h]).wait_recv()
         rows = jnp.concatenate([rows_in[pl.ds(pl.multiple_of(c * FETCH, PART), FETCH), :] for c in cells], axis=0)
-        second = lax.rem(lax.div(lax.broadcasted_iota(jnp.int32, (384, 1), 0), SLOT), 2) * FETCH
+        second = lax.rem(lax.div(lax.broadcasted_iota(jnp.int32, (SPAN, 1), 0), SLOT), WIDE) * FETCH
         left_rows = dot(one_hot(slot_columns(slot_a, i), D), left[...])
-        right_rows = dot(one_hot(slot_columns(slot_m, i).astype(jnp.int32) + second, 2 * FETCH), rows)
-        gate = gate_s[pl.ds(pl.multiple_of(i * 384, 128), 384), :]
+        right_rows = dot(one_hot(slot_columns(slot_m, i) + second.astype(F32), WIDE * FETCH), rows)
+        gate = gate_s[pl.ds(pl.multiple_of(i * SPAN, 128), SPAN), :]
         edge = (left_rows * right_rows * gate).astype(BF16)
         mixed = silu(dot(edge, w_mix[...])).astype(BF16)
         out = dot_nt(w_flip[...], mixed)
         for o in range(3):
-            top = out[0:HALF, o * 128:(o + 1) * 128]
-            bottom = out[HALF:2 * HALF, o * 128:(o + 1) * 128]
-            blk_out[2 * i, o] = jnp.where(low, top, pltpu.roll(bottom, SLOT, 1)).astype(BF16)
-            blk_out[2 * i + 1, o] = jnp.where(low, pltpu.roll(top, SLOT, 1), bottom).astype(BF16)
+            for h in range(0, WIDE, 2):
+                start = (o * WIDE + h) * SLOT
+                top = out[0:HALF, start:start + 128]
+                bottom = out[HALF:2 * HALF, start:start + 128]
+                blk_out[WIDE * i + h, o] = jnp.where(low, top, pltpu.roll(bottom, SLOT, 1)).astype(BF16)
+                blk_out[WIDE * i + h + 1, o] = jnp.where(low, pltpu.roll(top, SLOT, 1), bottom).astype(BF16)
 
         @pl.when(i > 0)
         def _():
@@ -307,13 +312,13 @@
     w_own[...] = w_out[0:2 * HALF, :]
     w_flip[...] = dot(jnp.where((entry < BLOCK) & (lane == flipped), 1.0, 0.0).astype(BF16), w_out[...]).astype(BF16)
 
-    lax.fori_loop(0, CELLS // 2, slots, 0)
+    lax.fori_loop(0, CELLS // WIDE, slots, 0)
 
     index = row_index(slot[...], prow[...])
     for source, target in ((dist[...], pair_d), (envelope_of(dist[...]), pair_e), (atom[...].astype(F32), pair_a), (index.astype(F32), pair_r)):
         square[0:32, :] = source
         target[...] = square[...].T
-    send_blocks_of(CELLS // 2 - 1)
+    send_blocks_of(CELLS // WIDE - 1)
 
     def pair_gates(j, _):
         d = jnp.concatenate([column(pair_d[...], 2 * j + h) for h in range(2)], axis=0)
@@ -321,7 +326,7 @@
         gate_o[pl.ds(pl.multiple_of(j * 256, 256), 256), :] = gate_of(d, e, w_rin[...], w_rout[...])
         return 0
 
-    lax.fori_loop(0, PAIRS // 256, pair_gates, 0)
+    lax.fori_loop(0, PAIRS // 256, pair_gates, 0, unroll=4)
 
     def pairs(j, _):
         index_l = jnp.concatenate([column(pair_a[...], 2 * j + h) for h in range(2)], axis=0)
@@ -334,7 +339,7 @@
         own[:, at] = dot_nt(w_own[...], mixed)[0:BLOCK].astype(BF16)
         return 0
 
-    lax.fori_loop(0, PAIRS // 256, pairs, 0)
+    lax.fori_loop(0, PAIRS // 256, pairs, 0, unroll=4)
 
     own_block.wait()
     block_copy(0, 0, me).wait()

time: 92.2 us -> 90.1 us (0.977)
  the two profiles are of different devices: /device:TPU:64 before, /device:TPU:9 now
where the time goes in v4:
time: 90.1 us; the launch traced here: 90 us
  Pallas kernels  89.4 us (99%)
    pallas_call x1, Pallas kernels, body(): pl.pallas_call(main_kernel, out_shape=outputs, in_specs=[hbm] * 12, out_s...  87.5 us
    pallas_call x1, Pallas kernels, body(): pl.pallas_call(output_kernel, out_shape=outputs, in_specs=[vmem, vmem], o...  1.83 us

profile of v4, /device:TPU:9, one launch (start us, length us, event | category | flops | bytes accessed | tf_op | source)
XLA Modules:
  0.0 90.0 jit_solution(2248181384564043112)
XLA Ops:
  0.6 87.5 %shard_map.131 = (bf16[169,4096]{1,0:T(8,128)(2,1)S(1)}, bf16[169,6144]{1,0:T(8,128)(2,1)S(1)}) custom-call(bf16[256,256]{1,0:T(8,128)(2,1)} %feat_h.1, s32[32,128]{1,0:T(8,128)} %bitcast.6, s32[32,128]{1,0:T(8,128)} %bitcast.7, s32[32,128]{1,0:T(8,128)} %bitcast.8, f32[32,128]{1,0:T(8,128)} %bitcast.9, s32[32,48]{1,0:T(8,128)} %lists_h.1, ...), custom_call_target="tpu_custom_call" | custom-call | tf_op jit(solution)/shard_map/pallas_call | solution.py:396
  88.2 1.8 %shard_map.132 = (bf16[169,4096]{1,0:T(8,128)(2,1)}, bf16[169,6144]{1,0:T(8,128)(2,1)}) custom-call(bf16[169,4096]{1,0:T(8,128)(2,1)S(1)} %get-tuple-element.4.own_in, bf16[169,6144]{1,0:T(8,128)(2,1)S(1)} %get-tuple-element.5.partner_in), custom_call_target="tpu_custom_call" | custom-call | tf_op jit(solution)/shard_map/pallas_call | solution.py:439

commit v5 on v4

--- a/solution.py
+++ b/solution.py
@@ -29,6 +29,10 @@
 EARLY = 2
 WIDE = 4
 SPAN = 3 * WIDE * SLOT
+NEAR = 5
+FAR = Z - NEAR
+NEAR_CELLS = NEAR * X
+FAR_CELLS = FAR * X
 
 
 def silu(x):
@@ -95,10 +99,10 @@
     feat_h, atom_h, prow_h, slot_h, dist_h, lists_h, w_left_h, w_right_h, w_rin_h, w_rout_h, w_mix_h, w_out_h,
     own, partner,
     feat, atom, prow, slot, dist, lists, w_left, w_right, w_rin, w_rout, w_mix, w_raw, w_out,
-    feat_in, tables, left, rows_out, rows_in, gate_s, gate_o, blk_out, blk_in,
-    slot_d, slot_e, slot_a, slot_m, pair_d, pair_e, pair_a, pair_r, list_t, list_s,
+    feat_in, list_in, far_f, scal_out, scal_in, tables, left, rows_out, rows_in, gate_s, gate_o, blk_out, blk_in,
+    slot_d, slot_e, slot_a, slot_m, pair_d, pair_e, pair_a, pair_r, list_t, list_s, list_n, turn_a, turn_b,
     square, w_own, w_flip,
-    in_sem, feat_ss, feat_rs, rows_ss, rows_rs, blk_ss, blk_rs, local_sem,
+    in_sem, feat_ss, feat_rs, list_ss, list_rs, hop_ss, hop_rs, side_ss, side_rs, near_ss, near_rs, scal_ss, scal_rs, rows_ss, rows_rs, blk_ss, blk_rs, local_sem,
 ):
     me = lax.axis_index("cell")
     sources = (feat_h, w_left_h, w_right_h, lists_h, slot_h, dist_h, atom_h, prow_h, w_out_h, w_rin_h, w_rout_h, w_mix_h)
@@ -171,6 +175,17 @@
     slot_e[...] = envelope_of(d)
     slot_a[...] = total[3 * SLOT:4 * SLOT] - 1.0
     slot_m[...] = total[4 * SLOT:5 * SLOT]
+    turn_a[...] = jnp.concatenate([d, total[3 * SLOT:4 * SLOT] - 1.0], axis=0).T
+    turn_b[...] = jnp.concatenate([total[4 * SLOT:5 * SLOT], jnp.zeros((SLOT, 128), F32)], axis=0).T
+
+    def pack_scalars(n, _):
+        c = cell_at(lax.rem(n, X) * Z + NEAR + lax.div(n, X), -1)
+        for o in range(3):
+            scal_out[3 * n + o, 0:1, :] = turn_a[pl.ds(o * CELLS + c, 1), :]
+            scal_out[3 * n + o, 1:2, :] = turn_b[pl.ds(o * CELLS + c, 1), :]
+        return 0
+
+    lax.fori_loop(0, FAR_CELLS, pack_scalars, 0)
 
     pl.semaphore_wait(barrier, 3 * CELLS - 1)
 
@@ -206,8 +221,46 @@
                 def _():
                     row_copy(8 * i, o, me).start()
 
+    def list_copy(which):
+        return pltpu.make_async_remote_copy(
+            src_ref=lists, dst_ref=list_in.at[which], send_sem=list_ss.at[which], recv_sem=list_rs.at[which],
+            device_id=(strip_at(1 - 2 * which), me), device_id_type=MESH,
+        )
+
+    def far_step(b, dx):
+        return dx * Z + NEAR + b
+
+    def hop_copy(b):
+        return pltpu.make_async_remote_copy(
+            src_ref=feat, dst_ref=far_f.at[1, b * X], send_sem=hop_ss.at[b], recv_sem=hop_rs.at[b],
+            device_id=(strip_at(0), cell_at(far_step(b, 0), -1)), device_id_type=MESH,
+        )
+
+    def side_copy(b, dx):
+        return pltpu.make_async_remote_copy(
+            src_ref=far_f.at[1, b * X], dst_ref=far_f.at[1, b * X + dx],
+            send_sem=side_ss.at[b, dx - 1], recv_sem=side_rs.at[b, dx - 1],
+            device_id=(strip_at(0), cell_at(dx * Z, -1)), device_id_type=MESH,
+        )
+
+    def near_copy(n, which):
+        return pltpu.make_async_remote_copy(
+            src_ref=far_f.at[1, n], dst_ref=far_f.at[2 * which, n],
+            send_sem=near_ss.at[n, which], recv_sem=near_rs.at[n, which],
+            device_id=(strip_at(1 - 2 * which), me), device_id_type=MESH,
+        )
+
+    def scalar_copy(n, o):
+        k = far_step(lax.div(n, X), lax.rem(n, X))
+        return pltpu.make_async_remote_copy(
+            src_ref=scal_out.at[3 * n + o], dst_ref=scal_in.at[3 * n + o],
+            send_sem=scal_ss.at[n, o], recv_sem=scal_rs.at[n, o],
+            device_id=(strip_at(o - 1), cell_at(k, -1)), device_id_type=MESH,
+        )
+
     for which in range(2):
         feature_copy(which).start()
+        list_copy(which).start()
 
     def send_own_part(i, _):
         send_rows_of(1, i)
@@ -215,8 +268,11 @@
 
     lax.fori_loop(0, CELLS // 8, send_own_part, 0)
 
+    def near_step(n):
+        return lax.div(n, NEAR) * Z + lax.rem(n, NEAR)
+
     def slot_columns(source, i):
-        cells = [cell_at(WIDE * i + h, -1) for h in range(WIDE)]
+        cells = [cell_at(near_step(WIDE * i + h), -1) for h in range(WIDE)]
         return jnp.concatenate([column(source[...], o * CELLS + c) for o in range(3) for c in cells], axis=0)
 
     def slot_gates(i, _):
@@ -243,7 +299,21 @@
     lax.fori_loop(0, CELLS // 4, pick_rest, 0)
     lax.fori_loop(early, early + 1, slot_gates, 0)
     send_rows_of(2, CELLS // 8 - 1)
-    lax.fori_loop(early + 1, CELLS // WIDE, slot_gates, 0)
+    for b in range(FAR):
+        hop_copy(b).start()
+
+    def send_scalars(n, _):
+        for o in range(3):
+            scalar_copy(n, o).start()
+        return 0
+
+    lax.fori_loop(0, FAR_CELLS, send_scalars, 0)
+    for which in range(2):
+        list_copy(which).wait()
+        square[0:32, 0:FETCH] = list_in[which].astype(F32)
+        list_t[...] = square[...].T
+        list_n[which] = list_t[pl.ds(2 - 2 * which, PART, stride=3), :] - float((2 - 2 * which) * D)
+    lax.fori_loop(early + 1, NEAR_CELLS // WIDE, slot_gates, 0)
 
     def block_copy(k, o, sender):
         return pltpu.make_async_remote_copy(
@@ -258,7 +328,7 @@
         for h in range(WIDE):
             for o in range(3):
                 if h or o != 1:
-                    block_copy(WIDE * i + h, o, me).start()
+                    block_copy(near_step(WIDE * i + h), o, me).start()
                 else:
                     @pl.when(i == 0)
                     def _():
@@ -266,12 +336,27 @@
 
                     @pl.when(i > 0)
                     def _():
-                        block_copy(WIDE * i, 1, me).start()
+                        block_copy(near_step(WIDE * i), 1, me).start()
 
     low = lax.broadcasted_iota(jnp.int32, (HALF, 128), 1) < SLOT
 
+    def halves(out, o, h):
+        start = (o * WIDE + h) * SLOT
+        top = out[0:HALF, start:start + 128]
+        bottom = out[HALF:2 * HALF, start:start + 128]
+        return (
+            jnp.where(low, top, pltpu.roll(bottom, SLOT, 1)).astype(BF16),
+            jnp.where(low, pltpu.roll(top, SLOT, 1), bottom).astype(BF16),
+        )
+
+    def far_rows(n, _):
+        k = far_step(lax.div(n, X), lax.rem(n, X))
+        for o in range(3):
+            row_copy(k, o, cell_at(k, -1)).wait_recv()
+        return 0
+
     def slots(i, _):
-        cells = [cell_at(WIDE * i + h, -1) for h in range(WIDE)]
+        cells = [cell_at(near_step(WIDE * i + h), -1) for h in range(WIDE)]
         for o in range(3):
             @pl.when(i == 0)
             def _():
@@ -279,9 +364,9 @@
 
             @pl.when(i > 0)
             def _():
-                row_copy(WIDE * i, o, cells[0]).wait_recv()
+                row_copy(near_step(WIDE * i), o, cells[0]).wait_recv()
             for h in range(1, WIDE):
-                row_copy(WIDE * i + h, o, cells[h]).wait_recv()
+                row_copy(near_step(WIDE * i + h), o, cells[h]).wait_recv()
         rows = jnp.concatenate([rows_in[pl.ds(pl.multiple_of(c * FETCH, PART), FETCH), :] for c in cells], axis=0)
         second = lax.rem(lax.div(lax.broadcasted_iota(jnp.int32, (SPAN, 1), 0), SLOT), WIDE) * FETCH
         left_rows = dot(one_hot(slot_columns(slot_a, i), D), left[...])
@@ -292,11 +377,9 @@
         out = dot_nt(w_flip[...], mixed)
         for o in range(3):
             for h in range(0, WIDE, 2):
-                start = (o * WIDE + h) * SLOT
-                top = out[0:HALF, start:start + 128]
-                bottom = out[HALF:2 * HALF, start:start + 128]
-                blk_out[WIDE * i + h, o] = jnp.where(low, top, pltpu.roll(bottom, SLOT, 1)).astype(BF16)
-                blk_out[WIDE * i + h + 1, o] = jnp.where(low, pltpu.roll(top, SLOT, 1), bottom).astype(BF16)
+                first, second = halves(out, o, h)
+                blk_out[near_step(WIDE * i + h), o] = first
+                blk_out[near_step(WIDE * i + h + 1), o] = second
 
         @pl.when(i > 0)
         def _():
@@ -312,13 +395,11 @@
     w_own[...] = w_out[0:2 * HALF, :]
     w_flip[...] = dot(jnp.where((entry < BLOCK) & (lane == flipped), 1.0, 0.0).astype(BF16), w_out[...]).astype(BF16)
 
-    lax.fori_loop(0, CELLS // WIDE, slots, 0)
-
     index = row_index(slot[...], prow[...])
     for source, target in ((dist[...], pair_d), (envelope_of(dist[...]), pair_e), (atom[...].astype(F32), pair_a), (index.astype(F32), pair_r)):
         square[0:32, :] = source
         target[...] = square[...].T
-    send_blocks_of(CELLS // WIDE - 1)
+
 
     def pair_gates(j, _):
         d = jnp.concatenate([column(pair_d[...], 2 * j + h) for h in range(2)], axis=0)
@@ -326,7 +407,11 @@
         gate_o[pl.ds(pl.multiple_of(j * 256, 256), 256), :] = gate_of(d, e, w_rin[...], w_rout[...])
         return 0
 
+
     lax.fori_loop(0, PAIRS // 256, pair_gates, 0, unroll=4)
+    lax.fori_loop(0, NEAR_CELLS // WIDE, slots, 0)
+    lax.fori_loop(0, FAR_CELLS, far_rows, 0)
+    send_blocks_of(NEAR_CELLS // WIDE - 1)
 
     def pairs(j, _):
         index_l = jnp.concatenate([column(pair_a[...], 2 * j + h) for h in range(2)], axis=0)
@@ -339,7 +424,37 @@
         own[:, at] = dot_nt(w_own[...], mixed)[0:BLOCK].astype(BF16)
         return 0
 
-    lax.fori_loop(0, PAIRS // 256, pairs, 0, unroll=4)
+    def to_sides(b):
+        hop_copy(b).wait_recv()
+        for dx in range(1, X):
+            side_copy(b, dx).start()
+        for which in range(2):
+            near_copy(b * X, which).start()
+
+    def to_strips(b):
+        for dx in range(1, X):
+            side_copy(b, dx).wait_recv()
+            for which in range(2):
+                near_copy(b * X + dx, which).start()
+
+    def pairs_of(i, _):
+        for h in range(4):
+            pairs(4 * i + h, 0)
+
+        @pl.when(i == 0)
+        def _():
+            to_sides(0)
+            to_sides(1)
+            to_sides(2)
+
+        @pl.when(i == 2)
+        def _():
+            to_strips(0)
+            to_strips(1)
+            to_strips(2)
+        return 0
+
+    lax.fori_loop(0, PAIRS // 1024, pairs_of, 0)
 
     own_block.wait()
     block_copy(0, 0, me).wait()
@@ -351,11 +466,12 @@
         x = lax.rem(lax.div(n, 3) + lax.div(me, Z), X)
         rank = lax.div(n, 3 * X)
         middle = lax.div(rank + 2, 3) * (1 + 2 * lax.rem(rank + parity, 2))
-        shift = middle * lax.div(3 - rank + 2, 3) + 2 * lax.div(rank, 3)
-        shift = lax.rem(shift, 4)
+        shift = lax.rem(middle * lax.div(3 - rank + 2, 3) + 2 * lax.div(rank, 3), 4)
         even = x * Z + 2 * lax.rem(lax.div(lax.rem(me, Z), 2) + shift, 4)
         for h in range(2):
-            @pl.when(even + h != me)
+            away = lax.rem(lax.rem(even, Z) + h - lax.rem(me, Z) + Z + 2, Z)
+
+            @pl.when((even + h != me) & (away < NEAR))
             def _():
                 block_copy(0, o, even + h).wait_recv()
         base = o * CELLS + even
@@ -366,15 +482,70 @@
         partner[:, pl.ds(pl.multiple_of(base * SLOT, 128), 128)] = jnp.concatenate([top, bottom], axis=0)[0:BLOCK].astype(BF16)
         return 0
 
-    lax.fori_loop(0, GROUPS // 2, unpack, 0)
+    def far(b, _):
+        groups = [(o, dx) for o in range(3) for dx in range(X)]
+        cells = [cell_at(far_step(b, dx), 1) for dx in range(X)]
+        for dx in range(X):
+            for which in range(2):
+                near_copy(b * X + dx, which).wait_recv()
+        for g, (o, dx) in enumerate(groups):
+            scalar_copy(b * X + dx, o).wait_recv()
+            turn_a[g:g + 1, :] = scal_in[3 * (b * X + dx) + o, 0:1, :]
+            turn_b[g:g + 1, :] = scal_in[3 * (b * X + dx) + o, 1:2, :]
+        square[0:16, :] = envelope_of(turn_a[0:16, :])
+        values, places, envelopes = turn_a[...].T, turn_b[...].T, square[...].T
+        d = jnp.concatenate([values[0:SLOT, g:g + 1] for g in range(12)], axis=0)
+        e = jnp.concatenate([envelopes[0:SLOT, g:g + 1] for g in range(12)], axis=0)
+        m = jnp.concatenate([places[0:SLOT, g:g + 1] + float((g - o) * PART) for g, (o, dx) in enumerate(groups)], axis=0)
+        gate = gate_of(d, e, w_rin[...], w_rout[...])
+        entries = (list_n[1], list_s[PART:2 * PART, :], list_n[0])
+        index = jnp.concatenate([column(entries[o], cells[dx]) for o, dx in groups], axis=0)
+        rows = dot(one_hot(index, D), tables[1]).astype(BF16)
+        right_rows = dot(one_hot(m, 12 * PART), rows)
+        picked = jnp.concatenate(
+            [dot(one_hot(values[SLOT:2 * SLOT, g:g + 1], D), far_f[2 - o, b * X + dx]).astype(BF16) for g, (o, dx) in enumerate(groups)], axis=0
+        )
+        left_rows = dot(picked, w_left[...]).astype(BF16).astype(F32)
+        edge = (left_rows * right_rows * gate).astype(BF16)
+        mixed = silu(dot(edge, w_mix[...])).astype(BF16)
+        out = dot_nt(w_flip[...], mixed)
+        for o in range(3):
+            for h in range(0, X, 2):
+                first, second = halves(out, o, h)
+                blk_in[o * CELLS + cells[h]] = first
+                blk_in[o * CELLS + cells[h + 1]] = second
+        return 0
+
+    lax.fori_loop(0, GROUPS // 4, unpack, 0)
+    lax.fori_loop(0, FAR, far, 0)
+    lax.fori_loop(GROUPS // 4, GROUPS // 2, unpack, 0)
 
     def finish(k, _):
         for o in range(3):
             row_copy(k, o, me).wait_send()
-            block_copy(k, o, me).wait_send()
         return 0
 
     lax.fori_loop(1, CELLS, finish, 0)
+
+    def finish_blocks(n, _):
+        for o in range(3):
+            block_copy(near_step(n), o, me).wait_send()
+        return 0
+
+    lax.fori_loop(1, NEAR_CELLS, finish_blocks, 0)
+
+    def finish_far(n, _):
+        for o in range(3):
+            scalar_copy(n, o).wait_send()
+        for which in range(2):
+            near_copy(n, which).wait_send()
+        return 0
+
+    lax.fori_loop(0, FAR_CELLS, finish_far, 0)
+    for b in range(FAR):
+        hop_copy(b).wait_send()
+        for dx in range(1, X):
+            side_copy(b, dx).wait_send()
 
 
 def output_kernel(own_in, partner_in, own, partner, sem):
@@ -411,6 +582,10 @@
             pltpu.VMEM((BLOCK, D), BF16),
             pltpu.VMEM((D, D), BF16),
             pltpu.VMEM((2, D, D), BF16),
+            pltpu.VMEM((2, CELLS, FETCH), jnp.int32),
+            pltpu.VMEM((3, FAR_CELLS, D, D), BF16),
+            pltpu.VMEM((3 * FAR_CELLS, 2, 128), F32),
+            pltpu.VMEM((3 * FAR_CELLS, 2, 128), F32),
             pltpu.VMEM((3, D, D), BF16),
             pltpu.VMEM((D, D), BF16),
             pltpu.VMEM((3, CELLS * PART, D), BF16),
@@ -422,10 +597,12 @@
             *[pltpu.VMEM((SLOT, 128), F32)] * 4,
             *[pltpu.VMEM((128, 128), F32)] * 5,
             pltpu.VMEM((FETCH, 128), F32),
-            pltpu.VMEM((128, 128), F32),
+            pltpu.VMEM((2, PART, 128), F32),
+            *[pltpu.VMEM((128, 128), F32)] * 3,
             pltpu.VMEM((2 * HALF, D), BF16),
             pltpu.VMEM((2 * HALF, D), BF16),
-            sem((12,)), sem((2,)), sem((2,)), sem((CELLS, 3)), sem((CELLS, 3)), sem((CELLS, 3)), sem((CELLS, 3)), sem((4,)),
+            sem((12,)), *[sem((2,))] * 4, *[sem((FAR,))] * 2, *[sem((FAR, X - 1))] * 2,
+            *[sem((FAR_CELLS, 2))] * 2, *[sem((FAR_CELLS, 3))] * 2, sem((CELLS, 3)), sem((CELLS, 3)), sem((CELLS, 3)), sem((CELLS, 3)), sem((4,)),
         ],
         compiler_params=pltpu.CompilerParams(collective_id=0, has_side_effects=True, vmem_limit_bytes=48 << 20),
     )(*[pltpu.with_memory_space_constraint(a, pltpu.HBM) for a in (

time: 90.1 us -> 95.4 us (1.059)
  the two profiles are of different devices: /device:TPU:9 before, /device:TPU:56 now
where the time goes in v5:
time: 95.4 us; the launch traced here: 95.3 us
  Pallas kernels  94.7 us (99%)
    pallas_call x1, Pallas kernels, body(): pl.pallas_call(main_kernel, out_shape=outputs, in_specs=[hbm] * 12, out_s...  92.8 us

profile of v5, /device:TPU:56, one launch (start us, length us, event | category | flops | bytes accessed | tf_op | source)
XLA Modules:
  0.0 95.3 jit_solution(16387331666367776836)
XLA Ops:
  0.6 92.8 %shard_map.131 = (bf16[169,4096]{1,0:T(8,128)(2,1)S(1)}, bf16[169,6144]{1,0:T(8,128)(2,1)S(1)}) custom-call(bf16[256,256]{1,0:T(8,128)(2,1)} %feat_h.1, s32[32,128]{1,0:T(8,128)} %bitcast.6, s32[32,128]{1,0:T(8,128)} %bitcast.7, s32[32,128]{1,0:T(8,128)} %bitcast.8, f32[32,128]{1,0:T(8,128)} %bitcast.9, s32[32,48]{1,0:T(8,128)} %lists_h.1, ...), custom_call_target="tpu_custom_call" | custom-call | tf_op jit(solution)/shard_map/pallas_call | solution.py:567
  93.5 1.8 %shard_map.132 = (bf16[169,4096]{1,0:T(8,128)(2,1)}, bf16[169,6144]{1,0:T(8,128)(2,1)}) custom-call(bf16[169,4096]{1,0:T(8,128)(2,1)S(1)} %get-tuple-element.4.own_in, bf16[169,6144]{1,0:T(8,128)(2,1)S(1)} %get-tuple-element.5.partner_in), custom_call_target="tpu_custom_call" | custom-call | tf_op jit(solution)/shard_map/pallas_call | solution.py:616

commit v6 on v5

--- a/solution.py
+++ b/solution.py
@@ -29,7 +29,7 @@
 EARLY = 2
 WIDE = 4
 SPAN = 3 * WIDE * SLOT
-NEAR = 5
+NEAR = 7
 FAR = Z - NEAR
 NEAR_CELLS = NEAR * X
 FAR_CELLS = FAR * X
@@ -41,9 +41,11 @@
 
 
 def offset_of(k):
-    j = lax.rem(k, Z)
+    late = lax.div(k, NEAR_CELLS)
+    n = k - late * NEAR_CELLS
+    j = (1 - late) * lax.rem(k, NEAR) + late * (NEAR + lax.div(n, X))
     hop = lax.div(j + 1, 2) * (2 * lax.rem(j, 2) - 1)
-    return lax.div(k, Z), hop
+    return (1 - late) * lax.div(k, NEAR) + late * lax.rem(n, X), hop
 
 
 def cell_at(k, sign):
@@ -179,7 +181,7 @@
     turn_b[...] = jnp.concatenate([total[4 * SLOT:5 * SLOT], jnp.zeros((SLOT, 128), F32)], axis=0).T
 
     def pack_scalars(n, _):
-        c = cell_at(lax.rem(n, X) * Z + NEAR + lax.div(n, X), -1)
+        c = cell_at(NEAR_CELLS + n, -1)
         for o in range(3):
             scal_out[3 * n + o, 0:1, :] = turn_a[pl.ds(o * CELLS + c, 1), :]
             scal_out[3 * n + o, 1:2, :] = turn_b[pl.ds(o * CELLS + c, 1), :]
@@ -199,7 +201,7 @@
         return pltpu.make_async_remote_copy(
             src_ref=rows_out.at[o, pl.ds(pl.multiple_of(k * PART, PART), PART)],
             dst_ref=rows_in.at[pl.ds(pl.multiple_of(me * FETCH + o * PART, PART), PART)],
-            send_sem=rows_ss.at[k, o], recv_sem=rows_rs.at[sender, o],
+            send_sem=rows_ss.at[o], recv_sem=rows_rs.at[sender, o],
             device_id=(strip_at(0), cell_at(k, 1)), device_id_type=MESH,
         )
 
@@ -228,7 +230,7 @@
         )
 
     def far_step(b, dx):
-        return dx * Z + NEAR + b
+        return NEAR_CELLS + b * X + dx
 
     def hop_copy(b):
         return pltpu.make_async_remote_copy(
@@ -240,13 +242,13 @@
         return pltpu.make_async_remote_copy(
             src_ref=far_f.at[1, b * X], dst_ref=far_f.at[1, b * X + dx],
             send_sem=side_ss.at[b, dx - 1], recv_sem=side_rs.at[b, dx - 1],
-            device_id=(strip_at(0), cell_at(dx * Z, -1)), device_id_type=MESH,
+            device_id=(strip_at(0), cell_at(dx * NEAR, -1)), device_id_type=MESH,
         )
 
     def near_copy(n, which):
         return pltpu.make_async_remote_copy(
             src_ref=far_f.at[1, n], dst_ref=far_f.at[2 * which, n],
-            send_sem=near_ss.at[n, which], recv_sem=near_rs.at[n, which],
+            send_sem=near_ss.at[which], recv_sem=near_rs.at[n, which],
             device_id=(strip_at(1 - 2 * which), me), device_id_type=MESH,
         )
 
@@ -254,13 +256,15 @@
         k = far_step(lax.div(n, X), lax.rem(n, X))
         return pltpu.make_async_remote_copy(
             src_ref=scal_out.at[3 * n + o], dst_ref=scal_in.at[3 * n + o],
-            send_sem=scal_ss.at[n, o], recv_sem=scal_rs.at[n, o],
+            send_sem=scal_ss.at[0], recv_sem=scal_rs.at[n, o],
             device_id=(strip_at(o - 1), cell_at(k, -1)), device_id_type=MESH,
         )
 
     for which in range(2):
         feature_copy(which).start()
         list_copy(which).start()
+    for b in range(FAR):
+        hop_copy(b).start()
 
     def send_own_part(i, _):
         send_rows_of(1, i)
@@ -269,7 +273,7 @@
     lax.fori_loop(0, CELLS // 8, send_own_part, 0)
 
     def near_step(n):
-        return lax.div(n, NEAR) * Z + lax.rem(n, NEAR)
+        return n
 
     def slot_columns(source, i):
         cells = [cell_at(near_step(WIDE * i + h), -1) for h in range(WIDE)]
@@ -288,20 +292,20 @@
         feature_copy(which).wait()
         tables[2 * which] = dot(feat_in[which], w_right[...]).astype(BF16)
 
+    def rest(i):
+        return 2 * lax.div(i, 4), lax.rem(i, 4)
+
     def pick_rest(i, _):
-        pick(2 * lax.div(i, 4), lax.rem(i, 4))
+        pick(*rest(i))
 
         @pl.when(i > 0)
         def _():
-            send_rows_of(2 * lax.div(i - 1, 4), lax.rem(i - 1, 4))
+            send_rows_of(*rest(i - 1))
         return 0
 
     lax.fori_loop(0, CELLS // 4, pick_rest, 0)
     lax.fori_loop(early, early + 1, slot_gates, 0)
     send_rows_of(2, CELLS // 8 - 1)
-    for b in range(FAR):
-        hop_copy(b).start()
-
     def send_scalars(n, _):
         for o in range(3):
             scalar_copy(n, o).start()
@@ -401,6 +405,19 @@
         target[...] = square[...].T
 
 
+    def to_sides(b):
+        hop_copy(b).wait_recv()
+        for dx in range(1, X):
+            side_copy(b, dx).start()
+        for which in range(2):
+            near_copy(b * X, which).start()
+
+    def to_strips(b):
+        for dx in range(1, X):
+            side_copy(b, dx).wait_recv()
+            for which in range(2):
+                near_copy(b * X + dx, which).start()
+
     def pair_gates(j, _):
         d = jnp.concatenate([column(pair_d[...], 2 * j + h) for h in range(2)], axis=0)
         e = jnp.concatenate([column(pair_e[...], 2 * j + h) for h in range(2)], axis=0)
@@ -409,6 +426,8 @@
 
 
     lax.fori_loop(0, PAIRS // 256, pair_gates, 0, unroll=4)
+    for b in range(FAR):
+        to_sides(b)
     lax.fori_loop(0, NEAR_CELLS // WIDE, slots, 0)
     lax.fori_loop(0, FAR_CELLS, far_rows, 0)
     send_blocks_of(NEAR_CELLS // WIDE - 1)
@@ -424,34 +443,13 @@
         own[:, at] = dot_nt(w_own[...], mixed)[0:BLOCK].astype(BF16)
         return 0
 
-    def to_sides(b):
-        hop_copy(b).wait_recv()
-        for dx in range(1, X):
-            side_copy(b, dx).start()
-        for which in range(2):
-            near_copy(b * X, which).start()
-
-    def to_strips(b):
-        for dx in range(1, X):
-            side_copy(b, dx).wait_recv()
-            for which in range(2):
-                near_copy(b * X + dx, which).start()
-
     def pairs_of(i, _):
         for h in range(4):
             pairs(4 * i + h, 0)
 
-        @pl.when(i == 0)
-        def _():
-            to_sides(0)
-            to_sides(1)
-            to_sides(2)
-
-        @pl.when(i == 2)
+        @pl.when(i == 3)
         def _():
             to_strips(0)
-            to_strips(1)
-            to_strips(2)
         return 0
 
     lax.fori_loop(0, PAIRS // 1024, pairs_of, 0)
@@ -469,7 +467,7 @@
         shift = lax.rem(middle * lax.div(3 - rank + 2, 3) + 2 * lax.div(rank, 3), 4)
         even = x * Z + 2 * lax.rem(lax.div(lax.rem(me, Z), 2) + shift, 4)
         for h in range(2):
-            away = lax.rem(lax.rem(even, Z) + h - lax.rem(me, Z) + Z + 2, Z)
+            away = lax.rem(lax.rem(even, Z) + h - lax.rem(me, Z) + Z + NEAR // 2, Z)
 
             @pl.when((even + h != me) & (away < NEAR))
             def _():
@@ -516,16 +514,21 @@
                 blk_in[o * CELLS + cells[h + 1]] = second
         return 0
 
-    lax.fori_loop(0, GROUPS // 4, unpack, 0)
+    lax.fori_loop(0, 3 * GROUPS // 8, unpack, 0)
     lax.fori_loop(0, FAR, far, 0)
-    lax.fori_loop(GROUPS // 4, GROUPS // 2, unpack, 0)
-
-    def finish(k, _):
-        for o in range(3):
-            row_copy(k, o, me).wait_send()
-        return 0
-
-    lax.fori_loop(1, CELLS, finish, 0)
+    lax.fori_loop(3 * GROUPS // 8, GROUPS // 2, unpack, 0)
+
+    sent = []
+    for o in range(3):
+        sent.append((rows_out.at[o, pl.ds(PART, (CELLS - 1) * PART)], rows_in.at[pl.ds(0, (CELLS - 1) * PART)], rows_ss.at[o], rows_rs.at[0, o]))
+    for which in range(2):
+        sent.append((far_f.at[1], far_f.at[2 * which], near_ss.at[which], near_rs.at[0, which]))
+    sent.append((scal_out, scal_in, scal_ss.at[0], scal_rs.at[0, 0]))
+    for source, target, send_sem, recv_sem in sent:
+        pltpu.make_async_remote_copy(
+            src_ref=source, dst_ref=target, send_sem=send_sem, recv_sem=recv_sem,
+            device_id=(strip_at(1), me), device_id_type=MESH,
+        ).wait_send()
 
     def finish_blocks(n, _):
         for o in range(3):
@@ -534,14 +537,6 @@
 
     lax.fori_loop(1, NEAR_CELLS, finish_blocks, 0)
 
-    def finish_far(n, _):
-        for o in range(3):
-            scalar_copy(n, o).wait_send()
-        for which in range(2):
-            near_copy(n, which).wait_send()
-        return 0
-
-    lax.fori_loop(0, FAR_CELLS, finish_far, 0)
     for b in range(FAR):
         hop_copy(b).wait_send()
         for dx in range(1, X):
@@ -602,7 +597,7 @@
             pltpu.VMEM((2 * HALF, D), BF16),
             pltpu.VMEM((2 * HALF, D), BF16),
             sem((12,)), *[sem((2,))] * 4, *[sem((FAR,))] * 2, *[sem((FAR, X - 1))] * 2,
-            *[sem((FAR_CELLS, 2))] * 2, *[sem((FAR_CELLS, 3))] * 2, sem((CELLS, 3)), sem((CELLS, 3)), sem((CELLS, 3)), sem((CELLS, 3)), sem((4,)),
+            sem((2,)), sem((FAR_CELLS, 2)), sem((1,)), sem((FAR_CELLS, 3)), sem((3,)), sem((CELLS, 3)), sem((CELLS, 3)), sem((CELLS, 3)), sem((4,)),
         ],
         compiler_params=pltpu.CompilerParams(collective_id=0, has_side_effects=True, vmem_limit_bytes=48 << 20),
     )(*[pltpu.with_memory_space_constraint(a, pltpu.HBM) for a in (

time: 95.4 us -> 84.5 us (0.89)
  the two profiles are of different devices: /device:TPU:56 before, /device:TPU:1 now
where the time goes in v6:
time: 84.5 us; the launch traced here: 83.8 us
  Pallas kernels  83.2 us (98%)
    pallas_call x1, Pallas kernels, body(): pl.pallas_call(main_kernel, out_shape=outputs, in_specs=[hbm] * 12, out_s...  81.3 us
    pallas_call x1, Pallas kernels, body(): pl.pallas_call(output_kernel, out_shape=outputs, in_specs=[vmem, vmem], o...  1.83 us

profile of v6, /device:TPU:1, one launch (start us, length us, event | category | flops | bytes accessed | tf_op | source)
XLA Modules:
  0.0 83.8 jit_solution(4405919278020224773)
XLA Ops:
  0.6 81.3 %shard_map.131 = (bf16[169,4096]{1,0:T(8,128)(2,1)S(1)}, bf16[169,6144]{1,0:T(8,128)(2,1)S(1)}) custom-call(bf16[256,256]{1,0:T(8,128)(2,1)} %feat_h.1, s32[32,128]{1,0:T(8,128)} %bitcast.6, s32[32,128]{1,0:T(8,128)} %bitcast.7, s32[32,128]{1,0:T(8,128)} %bitcast.8, f32[32,128]{1,0:T(8,128)} %bitcast.9, s32[32,48]{1,0:T(8,128)} %lists_h.1, ...), custom_call_target="tpu_custom_call" | custom-call | tf_op jit(solution)/shard_map/pallas_call | solution.py:562
  82.0 1.8 %shard_map.132 = (bf16[169,4096]{1,0:T(8,128)(2,1)}, bf16[169,6144]{1,0:T(8,128)(2,1)}) custom-call(bf16[169,4096]{1,0:T(8,128)(2,1)S(1)} %get-tuple-element.4.own_in, bf16[169,6144]{1,0:T(8,128)(2,1)S(1)} %get-tuple-element.5.partner_in), custom_call_target="tpu_custom_call" | custom-call | tf_op jit(solution)/shard_map/pallas_call | solution.py:611

commit v7 on v6

--- a/solution.py
+++ b/solution.py
@@ -101,10 +101,10 @@
     feat_h, atom_h, prow_h, slot_h, dist_h, lists_h, w_left_h, w_right_h, w_rin_h, w_rout_h, w_mix_h, w_out_h,
     own, partner,
     feat, atom, prow, slot, dist, lists, w_left, w_right, w_rin, w_rout, w_mix, w_raw, w_out,
-    feat_in, list_in, far_f, scal_out, scal_in, tables, left, rows_out, rows_in, gate_s, gate_o, blk_out, blk_in,
+    feat_in, list_in, far_f, scal_out, scal_in, entry_out, entry_in, tables, left, rows_out, rows_in, gate_s, gate_o, blk_out, blk_in,
     slot_d, slot_e, slot_a, slot_m, pair_d, pair_e, pair_a, pair_r, list_t, list_s, list_n, turn_a, turn_b,
     square, w_own, w_flip,
-    in_sem, feat_ss, feat_rs, list_ss, list_rs, hop_ss, hop_rs, side_ss, side_rs, near_ss, near_rs, scal_ss, scal_rs, rows_ss, rows_rs, blk_ss, blk_rs, local_sem,
+    in_sem, feat_ss, feat_rs, list_ss, list_rs, hop_ss, hop_rs, side_ss, side_rs, near_ss, near_rs, scal_ss, scal_rs, entry_ss, entry_rs, rows_ss, rows_rs, blk_ss, blk_rs, local_sem,
 ):
     me = lax.axis_index("cell")
     sources = (feat_h, w_left_h, w_right_h, lists_h, slot_h, dist_h, atom_h, prow_h, w_out_h, w_rin_h, w_rout_h, w_mix_h)
@@ -133,6 +133,9 @@
     left[...] = dot(feat[...], w_left[...]).astype(BF16)
     tables[1] = dot(feat[...], w_right[...]).astype(BF16)
 
+    entry_out[...] = jnp.zeros_like(entry_out)
+    for n in range(FAR_CELLS):
+        entry_out[n, 0:1, 0:FETCH] = lists[pl.ds(cell_at(NEAR_CELLS + n, -1), 1), :].astype(F32)
     square[...] = jnp.zeros_like(square)
     square[0:32, 0:FETCH] = lists[...].astype(F32)
     list_t[...] = square[...].T
@@ -212,7 +215,11 @@
 
     def send_rows_of(o, i):
         for h in range(8):
-            if h:
+            if h >= NEAR_CELLS % 8:
+                @pl.when(i < CELLS // 8 - 1)
+                def _():
+                    row_copy(8 * i + h, o, me).start()
+            elif h:
                 row_copy(8 * i + h, o, me).start()
             else:
                 @pl.when(i == 0)
@@ -260,9 +267,17 @@
             device_id=(strip_at(o - 1), cell_at(k, -1)), device_id_type=MESH,
         )
 
+    def entry_copy(n):
+        return pltpu.make_async_remote_copy(
+            src_ref=entry_out.at[n], dst_ref=entry_in.at[n], send_sem=entry_ss.at[n], recv_sem=entry_rs.at[n],
+            device_id=(strip_at(0), cell_at(NEAR_CELLS + n, -1)), device_id_type=MESH,
+        )
+
     for which in range(2):
         feature_copy(which).start()
         list_copy(which).start()
+    for n in range(FAR_CELLS):
+        entry_copy(n).start()
     for b in range(FAR):
         hop_copy(b).start()
 
@@ -352,12 +367,6 @@
             jnp.where(low, top, pltpu.roll(bottom, SLOT, 1)).astype(BF16),
             jnp.where(low, pltpu.roll(top, SLOT, 1), bottom).astype(BF16),
         )
-
-    def far_rows(n, _):
-        k = far_step(lax.div(n, X), lax.rem(n, X))
-        for o in range(3):
-            row_copy(k, o, cell_at(k, -1)).wait_recv()
-        return 0
 
     def slots(i, _):
         cells = [cell_at(near_step(WIDE * i + h), -1) for h in range(WIDE)]
@@ -399,12 +408,6 @@
     w_own[...] = w_out[0:2 * HALF, :]
     w_flip[...] = dot(jnp.where((entry < BLOCK) & (lane == flipped), 1.0, 0.0).astype(BF16), w_out[...]).astype(BF16)
 
-    index = row_index(slot[...], prow[...])
-    for source, target in ((dist[...], pair_d), (envelope_of(dist[...]), pair_e), (atom[...].astype(F32), pair_a), (index.astype(F32), pair_r)):
-        square[0:32, :] = source
-        target[...] = square[...].T
-
-
     def to_sides(b):
         hop_copy(b).wait_recv()
         for dx in range(1, X):
@@ -418,19 +421,43 @@
             for which in range(2):
                 near_copy(b * X + dx, which).start()
 
+
+    for b in range(FAR):
+        to_sides(b)
+    lax.fori_loop(0, NEAR_CELLS // WIDE, slots, 0)
+
+    index = row_index(slot[...], prow[...])
+    for source, target in ((dist[...], pair_d), (envelope_of(dist[...]), pair_e), (atom[...].astype(F32), pair_a), (index.astype(F32), pair_r)):
+        square[0:32, :] = source
+        target[...] = square[...].T
+
+
+    send_blocks_of(NEAR_CELLS // WIDE - 1)
+    for b in range(FAR):
+        to_strips(b)
+
     def pair_gates(j, _):
         d = jnp.concatenate([column(pair_d[...], 2 * j + h) for h in range(2)], axis=0)
         e = jnp.concatenate([column(pair_e[...], 2 * j + h) for h in range(2)], axis=0)
         gate_o[pl.ds(pl.multiple_of(j * 256, 256), 256), :] = gate_of(d, e, w_rin[...], w_rout[...])
         return 0
 
-
     lax.fori_loop(0, PAIRS // 256, pair_gates, 0, unroll=4)
-    for b in range(FAR):
-        to_sides(b)
-    lax.fori_loop(0, NEAR_CELLS // WIDE, slots, 0)
-    lax.fori_loop(0, FAR_CELLS, far_rows, 0)
-    send_blocks_of(NEAR_CELLS // WIDE - 1)
+
+    for n in range(FAR_CELLS):
+        entry_copy(n).wait()
+        square[n:n + 1, :] = entry_in[n, 0:1, :]
+        for which in range(2):
+            near_copy(n, which).wait_recv()
+    list_t[...] = square[...].T
+    spans = [list_t[pl.ds(o, PART, stride=3), :] - float(o * D) for o in range(3)]
+    chosen = jnp.concatenate(
+        [dot(one_hot(spans[o][:, n:n + 1], D), far_f[o, n]).astype(BF16) for n in range(FAR_CELLS) for o in range(3)], axis=0
+    )
+    chosen = dot(chosen, w_right[...]).astype(BF16)
+    for n in range(FAR_CELLS):
+        rows_in[pl.ds(pl.multiple_of(cell_at(NEAR_CELLS + n, 1) * FETCH, PART), FETCH), :] = chosen[n * FETCH:(n + 1) * FETCH]
+
 
     def pairs(j, _):
         index_l = jnp.concatenate([column(pair_a[...], 2 * j + h) for h in range(2)], axis=0)
@@ -447,9 +474,6 @@
         for h in range(4):
             pairs(4 * i + h, 0)
 
-        @pl.when(i == 3)
-        def _():
-            to_strips(0)
         return 0
 
     lax.fori_loop(0, PAIRS // 1024, pairs_of, 0)
@@ -483,9 +507,6 @@
     def far(b, _):
         groups = [(o, dx) for o in range(3) for dx in range(X)]
         cells = [cell_at(far_step(b, dx), 1) for dx in range(X)]
-        for dx in range(X):
-            for which in range(2):
-                near_copy(b * X + dx, which).wait_recv()
         for g, (o, dx) in enumerate(groups):
             scalar_copy(b * X + dx, o).wait_recv()
             turn_a[g:g + 1, :] = scal_in[3 * (b * X + dx) + o, 0:1, :]
@@ -520,7 +541,7 @@
 
     sent = []
     for o in range(3):
-        sent.append((rows_out.at[o, pl.ds(PART, (CELLS - 1) * PART)], rows_in.at[pl.ds(0, (CELLS - 1) * PART)], rows_ss.at[o], rows_rs.at[0, o]))
+        sent.append((rows_out.at[o, pl.ds(PART, (NEAR_CELLS - 1) * PART)], rows_in.at[pl.ds(0, (NEAR_CELLS - 1) * PART)], rows_ss.at[o], rows_rs.at[0, o]))
     for which in range(2):
         sent.append((far_f.at[1], far_f.at[2 * which], near_ss.at[which], near_rs.at[0, which]))
     sent.append((scal_out, scal_in, scal_ss.at[0], scal_rs.at[0, 0]))
@@ -581,6 +602,8 @@
             pltpu.VMEM((3, FAR_CELLS, D, D), BF16),
             pltpu.VMEM((3 * FAR_CELLS, 2, 128), F32),
             pltpu.VMEM((3 * FAR_CELLS, 2, 128), F32),
+            pltpu.VMEM((FAR_CELLS, 2, 128), F32),
+            pltpu.VMEM((FAR_CELLS, 2, 128), F32),
             pltpu.VMEM((3, D, D), BF16),
             pltpu.VMEM((D, D), BF16),
             pltpu.VMEM((3, CELLS * PART, D), BF16),
@@ -597,7 +620,7 @@
             pltpu.VMEM((2 * HALF, D), BF16),
             pltpu.VMEM((2 * HALF, D), BF16),
             sem((12,)), *[sem((2,))] * 4, *[sem((FAR,))] * 2, *[sem((FAR, X - 1))] * 2,
-            sem((2,)), sem((FAR_CELLS, 2)), sem((1,)), sem((FAR_CELLS, 3)), sem((3,)), sem((CELLS, 3)), sem((CELLS, 3)), sem((CELLS, 3)), sem((4,)),
+            sem((2,)), sem((FAR_CELLS, 2)), sem((1,)), sem((FAR_CELLS, 3)), sem((FAR_CELLS,)), sem((FAR_CELLS,)), sem((3,)), sem((CELLS, 3)), sem((CELLS, 3)), sem((CELLS, 3)), sem((4,)),
         ],
         compiler_params=pltpu.CompilerParams(collective_id=0, has_side_effects=True, vmem_limit_bytes=48 << 20),
     )(*[pltpu.with_memory_space_constraint(a, pltpu.HBM) for a in (

time: 84.5 us -> 83.5 us (0.988)
  Pallas kernels: 83.2 us -> 81.7 us
    pallas_call x1, Pallas kernels: 81.3 us -> 79.9 us  [body(): pl.pallas_call(main_kernel, out_shape=outputs, in_specs=[hbm] * 12, out_s...]
where the time goes in v7:
time: 83.5 us; the launch traced here: 82.3 us
  Pallas kernels  81.7 us (98%)
    pallas_call x1, Pallas kernels, body(): pl.pallas_call(main_kernel, out_shape=outputs, in_specs=[hbm] * 12, out_s...  79.9 us
    pallas_call x1, Pallas kernels, body(): pl.pallas_call(output_kernel, out_shape=outputs, in_specs=[vmem, vmem], o...  1.83 us

profile of v7, /device:TPU:1, one launch (start us, length us, event | category | flops | bytes accessed | tf_op | source)
XLA Modules:
  0.0 82.3 jit_solution(13520799273967711234)
XLA Ops:
  0.6 79.9 %shard_map.131 = (bf16[169,4096]{1,0:T(8,128)(2,1)S(1)}, bf16[169,6144]{1,0:T(8,128)(2,1)S(1)}) custom-call(bf16[256,256]{1,0:T(8,128)(2,1)} %feat_h.1, s32[32,128]{1,0:T(8,128)} %bitcast.6, s32[32,128]{1,0:T(8,128)} %bitcast.7, s32[32,128]{1,0:T(8,128)} %bitcast.8, f32[32,128]{1,0:T(8,128)} %bitcast.9, s32[32,48]{1,0:T(8,128)} %lists_h.1, ...), custom_call_target="tpu_custom_call" | custom-call | tf_op jit(solution)/shard_map/pallas_call | solution.py:583
  80.5 1.8 %shard_map.132 = (bf16[169,4096]{1,0:T(8,128)(2,1)}, bf16[169,6144]{1,0:T(8,128)(2,1)}) custom-call(bf16[169,4096]{1,0:T(8,128)(2,1)S(1)} %get-tuple-element.4.own_in, bf16[169,6144]{1,0:T(8,128)(2,1)S(1)} %get-tuple-element.5.partner_in), custom_call_target="tpu_custom_call" | custom-call | tf_op jit(solution)/shard_map/pallas_call | solution.py:634

commit v8 on v7

--- a/solution.py
+++ b/solution.py
@@ -26,7 +26,7 @@
 CUTOFF = 8.0
 COUNT = 128
 PART = 16
-EARLY = 2
+EARLY = 4
 WIDE = 4
 SPAN = 3 * WIDE * SLOT
 NEAR = 7
@@ -115,7 +115,8 @@
 
     barrier = pltpu.get_barrier_semaphore()
 
-    def greet(k, _):
+    def greet(n, _):
+        k = CELLS - 1 - n
         c = cell_at(k, 1)
         for step in (-1, 0, 1):
             if step:
@@ -308,7 +309,7 @@
         tables[2 * which] = dot(feat_in[which], w_right[...]).astype(BF16)
 
     def rest(i):
-        return 2 * lax.div(i, 4), lax.rem(i, 4)
+        return 2 * lax.rem(i, 2), lax.div(i, 2)
 
     def pick_rest(i, _):
         pick(*rest(i))
@@ -485,8 +486,8 @@
 
     def unpack(n, _):
         o = lax.rem(n, 3)
-        x = lax.rem(lax.div(n, 3) + lax.div(me, Z), X)
-        rank = lax.div(n, 3 * X)
+        x = lax.rem(lax.div(n, 12) + lax.div(me, Z), X)
+        rank = lax.rem(lax.div(n, 3), X)
         middle = lax.div(rank + 2, 3) * (1 + 2 * lax.rem(rank + parity, 2))
         shift = lax.rem(middle * lax.div(3 - rank + 2, 3) + 2 * lax.div(rank, 3), 4)
         even = x * Z + 2 * lax.rem(lax.div(lax.rem(me, Z), 2) + shift, 4)
@@ -535,9 +536,8 @@
                 blk_in[o * CELLS + cells[h + 1]] = second
         return 0
 
-    lax.fori_loop(0, 3 * GROUPS // 8, unpack, 0)
     lax.fori_loop(0, FAR, far, 0)
-    lax.fori_loop(3 * GROUPS // 8, GROUPS // 2, unpack, 0)
+    lax.fori_loop(0, GROUPS // 2, unpack, 0)
 
     sent = []
     for o in range(3):

time: 83.5 us -> 79.2 us (0.949); the launches traced: 82.3 us -> 79.1 us
  Pallas kernels: 81.7 us -> 78.4 us
    pallas_call x1, Pallas kernels: 79.9 us -> 76.6 us  [body(): pl.pallas_call(main_kernel, out_shape=outputs, in_specs=[hbm] * 12, out_s...]
where the time goes in v8:
time: 79.2 us; the launch traced here: 79.1 us
  Pallas kernels  78.4 us (99%)
    pallas_call x1, Pallas kernels, body(): pl.pallas_call(main_kernel, out_shape=outputs, in_specs=[hbm] * 12, out_s...  76.6 us
    pallas_call x1, Pallas kernels, body(): pl.pallas_call(output_kernel, out_shape=outputs, in_specs=[vmem, vmem], o...  1.83 us

profile of v8, /device:TPU:1, one launch (start us, length us, event | category | flops | bytes accessed | tf_op | source)
XLA Modules:
  0.0 79.1 jit_solution(14108952104837286640)
XLA Ops:
  0.6 76.6 %shard_map.131 = (bf16[169,4096]{1,0:T(8,128)(2,1)S(1)}, bf16[169,6144]{1,0:T(8,128)(2,1)S(1)}) custom-call(bf16[256,256]{1,0:T(8,128)(2,1)} %feat_h.1, s32[32,128]{1,0:T(8,128)} %bitcast.6, s32[32,128]{1,0:T(8,128)} %bitcast.7, s32[32,128]{1,0:T(8,128)} %bitcast.8, f32[32,128]{1,0:T(8,128)} %bitcast.9, s32[32,48]{1,0:T(8,128)} %lists_h.1, ...), custom_call_target="tpu_custom_call" | custom-call | tf_op jit(solution)/shard_map/pallas_call | solution.py:583
  77.2 1.8 %shard_map.132 = (bf16[169,4096]{1,0:T(8,128)(2,1)}, bf16[169,6144]{1,0:T(8,128)(2,1)}) custom-call(bf16[169,4096]{1,0:T(8,128)(2,1)S(1)} %get-tuple-element.4.own_in, bf16[169,6144]{1,0:T(8,128)(2,1)S(1)} %get-tuple-element.5.partner_in), custom_call_target="tpu_custom_call" | custom-call | tf_op jit(solution)/shard_map/pallas_call | solution.py:634

commit v9 on v8

--- a/solution.py
+++ b/solution.py
@@ -537,7 +537,7 @@
         return 0
 
     lax.fori_loop(0, FAR, far, 0)
-    lax.fori_loop(0, GROUPS // 2, unpack, 0)
+    lax.fori_loop(0, GROUPS // 2, unpack, 0, unroll=2)
 
     sent = []
     for o in range(3):

time: 79.2 us -> 79.2 us (level)
  no operation moved by 1% of the time
where the time goes in v9:
time: 79.2 us; the launch traced here: 79.1 us
  Pallas kernels  78.4 us (99%)
    pallas_call x1, Pallas kernels, body(): pl.pallas_call(main_kernel, out_shape=outputs, in_specs=[hbm] * 12, out_s...  76.6 us
    pallas_call x1, Pallas kernels, body(): pl.pallas_call(output_kernel, out_shape=outputs, in_specs=[vmem, vmem], o...  1.83 us

profile of v9, /device:TPU:1, one launch (start us, length us, event | category | flops | bytes accessed | tf_op | source)
XLA Modules:
  0.0 79.1 jit_solution(605058217936487026)
XLA Ops:
  0.6 76.6 %shard_map.131 = (bf16[169,4096]{1,0:T(8,128)(2,1)S(1)}, bf16[169,6144]{1,0:T(8,128)(2,1)S(1)}) custom-call(bf16[256,256]{1,0:T(8,128)(2,1)} %feat_h.1, s32[32,128]{1,0:T(8,128)} %bitcast.6, s32[32,128]{1,0:T(8,128)} %bitcast.7, s32[32,128]{1,0:T(8,128)} %bitcast.8, f32[32,128]{1,0:T(8,128)} %bitcast.9, s32[32,48]{1,0:T(8,128)} %lists_h.1, ...), custom_call_target="tpu_custom_call" | custom-call | tf_op jit(solution)/shard_map/pallas_call | solution.py:583
  77.2 1.8 %shard_map.132 = (bf16[169,4096]{1,0:T(8,128)(2,1)}, bf16[169,6144]{1,0:T(8,128)(2,1)}) custom-call(bf16[169,4096]{1,0:T(8,128)(2,1)S(1)} %get-tuple-element.4.own_in, bf16[169,6144]{1,0:T(8,128)(2,1)S(1)} %get-tuple-element.5.partner_in), custom_call_target="tpu_custom_call" | custom-call | tf_op jit(solution)/shard_map/pallas_call | solution.py:634
